TPU v7x, 128 devices: a whole 4x4x4 slice. The times are simulated.
128 devices in a mesh: row: 8 (over y, core), col: 16 (over x, z).
Axes of the slice: x: 4, y: 4, z: 4, core: 2. Of those that a mesh axis runs over, the one named last changes fastest.
Arguments:
- river_lower: float32 [128, 2, 2, 16384], P('row', None, None, 'col'), may hold values from -1.3 to 0.6, as said below
- river_main: float32 [128, 2, 2, 16384], P('row', None, None, 'col'), may hold values from -0.9 to 2.01
- river_upper: float32 [128, 2, 2, 16384], P('row', None, None, 'col'), may hold values from -1.3 to 0.6
- river_rhs: float32 [128, 2, 16384], P('row', None, 'col'), may hold values from -0.08 to 0.08
- weir_crest: float32 [128, 16384], P('row', 'col'), may hold values from -1 to 1
- weir_regime: int32 [128, 16384], P('row', 'col'), may hold values from 0 to 2
- weir_tile: int32 [8, 16, 16, 1024, 1], P('row', 'col'), may hold values from 0 to 127; in each aligned block of 16384 rows (0 to 16383, 16384 to 32767, ..., all dimensions but the last counted through in order) at most 256 rows name the same one
- weir_row: int32 [128, 16384], P('row', 'col'), may hold values from 0 to 31
- weir_col: int32 [128, 16384], P('row', 'col'), may hold values from 0 to 511
- bed_level: float32 [256, 8192], P('row', 'col'), may hold values from -1 to 0
- water_depth: float32 [256, 8192], P('row', 'col'), may hold values from 0.02 to 1.5
- flux_first: float32 [256, 8192], P('row', 'col'), may hold values from -2.4 to 2.4
- flux_second: float32 [256, 8192], P('row', 'col'), may hold values from -2.4 to 2.4
- wet_mask: int32 [256, 8192], P('row', 'col'), may hold values 0 or 1
Outputs:
- river_state: float32 [128, 2, 16384], P('row', None, 'col')
- depth_out: float32 [256, 8192], P('row', 'col')
- first_out: float32 [256, 8192], P('row', 'col')
- second_out: float32 [256, 8192], P('row', 'col')
Inputs may be any that keep to these rules, and one draw needn't show every extreme that they name: `river_lower`: together with river_main and river_upper, the block matrix of each chain has a positive definite symmetric part. Of the weirs in one device's block weir_tile[r, c], at most 256 feed the same tile, and in some device's block a tile is fed by exactly 256.
All inputs are finite; a program needn't handle non-finite values. No bound on the sum of `wet_mask` on one device may be relied on, other than what follows from the above.
Results may differ from a plain program's by a relative error of at most 0.0003.
Values sent between devices are 32-bit elements; how exact they have to be, the bound alone decides.
A program may use at most 64 MiB of HBM per device.

v0:
```python
import functools

import jax
import jax.numpy as jnp
from jax import lax
from jax.experimental import pallas as pl
from jax.experimental.pallas import tpu as pltpu
from jax.sharding import PartitionSpec as P

GRAVITY = 9.81
TIME_STEP = 1.0
CELL_WIDTH = 10.0
MANNING_SQ = 0.0009
DEPTH_FLOOR = 0.05
WEIR_GAIN = 0.5
FREE_COEF = 0.5
SUB_COEF = 0.4
SUB_OFFSET = 0.25
GATE_COEF = 0.2
LANES = 128
SUB = 8
MESH = pl.DeviceIdType.MESH
VMEM_SPEC = pl.BlockSpec(memory_space=pltpu.VMEM)
f32 = jnp.float32
bf16 = jnp.bfloat16
i32 = jnp.int32


def mat_mat(a, b):
    return [
        a[0] * b[0] + a[1] * b[2],
        a[0] * b[1] + a[1] * b[3],
        a[2] * b[0] + a[3] * b[2],
        a[2] * b[1] + a[3] * b[3],
    ]


def mat_vec(a, v):
    return [a[0] * v[0] + a[1] * v[1], a[2] * v[0] + a[3] * v[1]]


def minus(a, b):
    return [x - y for x, y in zip(a, b)]


def plus(a, b):
    return [x + y for x, y in zip(a, b)]


def negative(a):
    return [-x for x in a]


def inverse(m):
    scale = 1.0 / (m[0] * m[3] - m[1] * m[2])
    return [m[3] * scale, -(m[1] * scale), -(m[2] * scale), m[0] * scale]


def river_kernel(
    n_row, sections, lower_ref, main_ref, upper_ref, rhs_ref, crest_ref, regime_ref,
    state_ref, keep_ref, slope_ref,
    couple, local, held, heads, head_in, edges, edge_in, crest, regime,
    send_one, recv_one, send_two, recv_two,
):
    me = lax.axis_index("row")
    barrier = pltpu.get_barrier_semaphore()
    for k in range(1, n_row):
        pl.semaphore_signal(
            barrier, inc=1, device_id={"row": lax.rem(me + k, n_row)}, device_id_type=MESH
        )

    def pair(ref, s, i, j):
        return ref[s, i, pl.ds(j, SUB, stride=2), :]

    def block(ref, s):
        return [pair(ref, s, i, j) for i in range(2) for j in range(2)]

    coupled = value = spike = None
    for s in range(sections):
        low, main, up = block(lower_ref, s), block(main_ref, s), block(upper_ref, s)
        right = [rhs_ref[s, pl.ds(j, SUB, stride=2), :] for j in range(2)]
        if s == 0:
            inv = inverse(main)
            value = mat_vec(inv, right)
            spike = negative(mat_mat(inv, low))
        else:
            inv = inverse(minus(main, mat_mat(low, coupled)))
            value = mat_vec(inv, minus(right, mat_vec(low, value)))
            spike = negative(mat_mat(inv, mat_mat(low, spike)))
        coupled = mat_mat(inv, up)
        for q in range(4):
            couple[s, q] = coupled[q]
            local[s, 2 + q] = spike[q]
        for q in range(2):
            local[s, q] = value[q]
    after = negative(coupled)
    for q in range(4):
        local[sections - 1, 6 + q] = after[q]
    tail = [value, spike, after]
    for s in range(sections - 2, -1, -1):
        here = [couple[s, q] for q in range(4)]
        value = minus([local[s, q] for q in range(2)], mat_vec(here, value))
        spike = minus([local[s, 2 + q] for q in range(4)], mat_mat(here, spike))
        after = negative(mat_mat(here, after))
        for q in range(2):
            local[s, q] = value[q]
        for q in range(4):
            local[s, 2 + q] = spike[q]
            local[s, 6 + q] = after[q]
    faces = value + spike + after + tail[0] + tail[1] + tail[2]
    for q, face in enumerate(faces):
        heads[:, q, :] = face

    pl.semaphore_wait(barrier, n_row - 1)
    copies = []
    for k in range(1, n_row):
        peer = lax.rem(me + k, n_row)
        copy = pltpu.make_async_remote_copy(
            src_ref=heads.at[peer], dst_ref=head_in.at[me],
            send_sem=send_one.at[k - 1], recv_sem=recv_one.at[k - 1],
            device_id={"row": peer}, device_id_type=MESH,
        )
        copy.start()
        copies.append(copy)
    head_in[me] = heads[me]
    for half in range(sections // SUB):
        for k in range(SUB):
            rows, cols = pl.ds(half * SUB, SUB), pl.ds(k * LANES, LANES)
            crest[rows, k, :] = crest_ref[rows, cols]
            regime[rows, k, :] = regime_ref[rows, cols]
    for copy in copies:
        copy.wait()

    def row(p, q):
        return head_in[p, q : q + 1, :]

    zero = jnp.zeros((1, LANES), f32)
    one = jnp.ones((1, LANES), f32)
    prev_couple, prev_value = [zero] * 4, [zero] * 2
    done = []
    for p in range(n_row):
        part = [row(p, q) for q in range(20)]
        head_y, head_l, head_r = part[0:2], part[2:6], part[6:10]
        tail_y, tail_l, tail_r = part[10:12], part[12:16], part[16:20]
        inv = inverse(plus([one, zero, zero, one], mat_mat(head_l, prev_couple)))
        first_couple = negative(mat_mat(inv, head_r))
        first_value = mat_vec(inv, plus(head_y, mat_vec(head_l, prev_value)))
        bridge = mat_mat(tail_l, prev_couple)
        last_couple = minus(negative(tail_r), mat_mat(bridge, first_couple))
        last_value = minus(plus(tail_y, mat_vec(tail_l, prev_value)), mat_vec(bridge, first_value))
        done.append((first_couple, first_value, last_couple, last_value))
        prev_couple, prev_value = last_couple, last_value
    following = [zero] * 2
    for p in range(n_row - 1, -1, -1):
        first_couple, first_value, last_couple, last_value = done[p]
        for q in range(2):
            edges[p, 2 + q : 3 + q, :] = following[q]
        last = minus(last_value, mat_vec(last_couple, following))
        if p + 1 < n_row:
            for q in range(2):
                edges[p + 1, q : q + 1, :] = last[q]
        following = minus(first_value, mat_vec(first_couple, following))
    for q in range(2):
        edges[0, q : q + 1, :] = zero
    copies = []
    for k in range(1, n_row):
        peer = lax.rem(me + k, n_row)
        copy = pltpu.make_async_remote_copy(
            src_ref=edges.at[peer], dst_ref=edge_in.at[me],
            send_sem=send_two.at[k - 1], recv_sem=recv_two.at[k - 1],
            device_id={"row": peer}, device_id_type=MESH,
        )
        copy.start()
        copies.append(copy)
    edge_in[me] = edges[me]
    for copy in copies:
        copy.wait()
    before = [edge_in[:, q, :] for q in range(2)]
    behind = [edge_in[:, 2 + q, :] for q in range(2)]
    for s in range(sections):
        solved = [local[s, q] for q in range(2)]
        solved = plus(solved, mat_vec([local[s, 2 + q] for q in range(4)], before))
        solved = plus(solved, mat_vec([local[s, 6 + q] for q in range(4)], behind))
        for j in range(2):
            state_ref[s, pl.ds(j, SUB, stride=2), :] = solved[j]
        phase = solved[0]
        head = jnp.maximum(phase - crest[s], 0.0)
        kind = regime[s]
        free = jnp.where(kind == 0, FREE_COEF * head * jnp.sqrt(head), 0.0)
        slope = jnp.where(
            kind == 1,
            SUB_COEF * jnp.sqrt(head + SUB_OFFSET),
            jnp.where(kind == 2, GATE_COEF, 0.0),
        )
        keep_ref[s] = WEIR_GAIN * (free + slope * phase)
        slope_ref[s] = WEIR_GAIN * slope


def solve_river(lower, main, upper, rhs, crest, regime, n_row):
    sections, chains = rhs.shape[0], rhs.shape[-1]

    def dense(x):
        x = x.reshape(x.shape[:-1] + (SUB, LANES))
        x = jnp.swapaxes(x, -2, -3)
        return x.reshape(x.shape[:-3] + (2 * SUB, LANES))

    wide = lambda *lead: pltpu.VMEM(lead + (SUB, LANES), f32)
    dma = pltpu.SemaphoreType.DMA((n_row - 1,))
    state, keep, slope = pl.pallas_call(
        functools.partial(river_kernel, n_row, sections),
        out_shape=(
            jax.ShapeDtypeStruct((sections, 2 * SUB, LANES), f32),
            jax.ShapeDtypeStruct((sections, SUB, LANES), f32),
            jax.ShapeDtypeStruct((sections, SUB, LANES), f32),
        ),
        in_specs=[VMEM_SPEC] * 6,
        out_specs=(VMEM_SPEC,) * 3,
        scratch_shapes=[
            wide(sections, 4), wide(sections, 10), wide(1),
            pltpu.VMEM((n_row, 24, LANES), f32), pltpu.VMEM((n_row, 24, LANES), f32),
            wide(n_row), wide(n_row),
            wide(sections), pltpu.VMEM((sections, SUB, LANES), i32),
            dma, dma, dma, dma,
        ],
        compiler_params=pltpu.CompilerParams(collective_id=0, has_side_effects=True),
        name="river",
    )(dense(lower), dense(main), dense(upper), dense(rhs), crest, regime)
    state = state.reshape(sections, SUB, 2, LANES)
    state = jnp.swapaxes(state, 1, 2).reshape(sections, 2, chains)
    return state, keep.reshape(-1, LANES), slope.reshape(-1, LANES)


STEP = 1024
PIECES = 6


def split_two(x):
    high = x.astype(bf16)
    return high, (x - high.astype(f32)).astype(bf16)


def fill_kernel(
    devices, capacity, tile_ref, row_ref, col_ref, keep_ref, slope_ref, out_ref,
    cell_one, cell_two, left, right, total, earlier,
):
    sections = row_ref.shape[0]
    for half in range(sections // SUB):
        for k in range(SUB):
            rows, cols = pl.ds(half * SUB, SUB), pl.ds(k * LANES, LANES)
            row, col = row_ref[rows, cols], col_ref[rows, cols]
            cell_one[rows, k, :] = (row + (col >> 8) * 32).astype(f32)
            cell_two[rows, k, :] = (col & 255).astype(f32)
    total[...] = jnp.zeros_like(total)
    width = 2 * LANES
    earlier[...] = (
        lax.broadcasted_iota(i32, (width, width), 0) < lax.broadcasted_iota(i32, (width, width), 1)
    ).astype(f32).astype(bf16)
    ones = jnp.ones((width, LANES), bf16)
    tile_table = lax.broadcasted_iota(i32, (devices, width), 0)
    rank_table = lax.broadcasted_iota(i32, (capacity, width), 0).astype(f32)

    def wide(ref, r):
        return jnp.concatenate([ref[r : r + 1, :], ref[r + 1 : r + 2, :]], axis=1)

    def step(index, offset):
        rows = pl.ds(pl.multiple_of(index * SUB, SUB), SUB)
        tiles = tile_ref[rows, :]
        keep, slope = keep_ref[rows, :], slope_ref[rows, :]
        ones_at, twos_at = cell_one[index], cell_two[index]
        values = split_two(keep) + split_two(slope) + (ones_at.astype(bf16), twos_at.astype(bf16))
        values = [v.astype(f32) for v in values]
        for part in range(STEP // width):
            tile = wide(tiles, 2 * part)
            hot = tile == tile_table
            hot_one = jnp.where(hot, 1.0, 0.0).astype(bf16)
            within = jnp.dot(hot_one, earlier[...], preferred_element_type=f32)
            counts = jnp.dot(hot_one, ones, preferred_element_type=f32)
            base = within + jnp.concatenate([offset, offset], axis=1)
            rank = jnp.sum(jnp.where(hot, base, 0.0), axis=0, keepdims=True)
            offset = offset + counts
            lanes = pl.ds(part * width, width)
            right[:, lanes] = jnp.where(rank == rank_table, 1.0, 0.0).astype(bf16)
            for q in range(PIECES):
                left[pl.ds(q * devices, devices), lanes] = jnp.where(
                    hot, wide(values[q], 2 * part), 0.0
                ).astype(bf16)
        total[...] += lax.dot_general(
            left[...], right[...], (((1,), (1,)), ((), ())), preferred_element_type=f32
        )
        return offset

    lax.fori_loop(0, tile_ref.shape[0] // SUB, step, jnp.zeros((devices, LANES), f32))
    piece = lambda q: total[pl.ds(q * devices, devices), :]
    out_ref[0] = piece(0) + piece(1)
    out_ref[1] = piece(2) + piece(3)
    out_ref[2] = piece(4) * 256.0 + piece(5)


def fill_slots(tile, row, col, keep, slope, devices, capacity):
    sections = row.shape[0]
    return pl.pallas_call(
        functools.partial(fill_kernel, devices, capacity),
        out_shape=jax.ShapeDtypeStruct((3, devices, capacity), f32),
        in_specs=[VMEM_SPEC] * 5,
        out_specs=VMEM_SPEC,
        scratch_shapes=[
            pltpu.VMEM((sections, SUB, LANES), f32), pltpu.VMEM((sections, SUB, LANES), f32),
            pltpu.VMEM((PIECES * devices, STEP), bf16), pltpu.VMEM((capacity, STEP), bf16),
            pltpu.VMEM((PIECES * devices, capacity), f32),
            pltpu.VMEM((2 * LANES, 2 * LANES), bf16),
        ],
        name="fill",
    )(tile, row, col, keep, slope)


def apply_kernel(in_ref, bed_ref, depth_ref, out_ref, left, right, total):
    sources, capacity = in_ref.shape[1:]
    height = depth_ref.shape[0]
    cells_one, cells_two = 2 * height, 256
    total[...] = jnp.zeros_like(total)
    one_table = lax.broadcasted_iota(i32, (cells_one, capacity), 0).astype(f32)
    two_table = lax.broadcasted_iota(i32, (cells_two, capacity), 0).astype(f32)
    group = SUB

    def step(index, carry):
        rows = pl.ds(pl.multiple_of(index * group, group), group)
        cell = in_ref[2, rows, :]
        first = jnp.floor(cell * (1.0 / 256.0))
        second = cell - first * 256.0
        values = split_two(in_ref[0, rows, :]) + split_two(in_ref[1, rows, :])
        values = [v.astype(f32) for v in values]
        for part in range(group):
            one = lambda v: v[part : part + 1, :]
            lanes = pl.ds(part * capacity, capacity)
            hot = one(first) == one_table
            right[:, lanes] = jnp.where(one(second) == two_table, 1.0, 0.0).astype(bf16)
            for q in range(4):
                left[pl.ds(q * cells_one, cells_one), lanes] = jnp.where(
                    hot, one(values[q]), 0.0
                ).astype(bf16)
        total[...] += lax.dot_general(
            left[...], right[...], (((1,), (1,)), ((), ())), preferred_element_type=f32
        )
        return carry

    lax.fori_loop(0, sources // group, step, 0)
    piece = lambda q, side: total[pl.ds(q * cells_one + side * height, height), :]
    for side in range(2):
        cols = pl.ds(side * cells_two, cells_two)
        keep = piece(0, side) + piece(1, side)
        slope = piece(2, side) + piece(3, side)
        depth = depth_ref[:, cols]
        surface = bed_ref[:, cols] + depth
        out_ref[:, cols] = jnp.maximum(depth + (keep - slope * surface), 0.0)


def apply_weirs(arrived, bed, depth):
    capacity = arrived.shape[2]
    return pl.pallas_call(
        apply_kernel,
        out_shape=jax.ShapeDtypeStruct(depth.shape, f32),
        in_specs=[VMEM_SPEC] * 3,
        out_specs=VMEM_SPEC,
        scratch_shapes=[
            pltpu.VMEM((256, SUB * capacity), bf16), pltpu.VMEM((256, SUB * capacity), bf16),
            pltpu.VMEM((256, 256), f32),
        ],
        name="apply",
    )(arrived, bed, depth)


def flood_kernel(
    n_row, n_col, height, width, depth_ref, bed_ref, one_ref, two_ref, mask_ref,
    depth_out, one_out, two_out, field, send, recv,
):
    my_row, my_col = lax.axis_index("row"), lax.axis_index("col")
    barrier = pltpu.get_barrier_semaphore()
    around = [(a, b) for a in (-1, 0, 1) for b in (-1, 0, 1) if (a, b) != (0, 0)]

    def device(a, b):
        return (lax.rem(my_row + a + n_row, n_row), lax.rem(my_col + b + n_col, n_col))

    for a, b in around:
        pl.semaphore_signal(barrier, inc=1, device_id=device(a, b), device_id_type=MESH)
    inner = (pl.ds(SUB, height), pl.ds(LANES, width))
    for q, ref in enumerate((depth_ref, bed_ref, one_ref, two_ref)):
        field[(q,) + inner] = ref[...]
    field[(4,) + inner] = mask_ref[...].astype(f32)
    pl.semaphore_wait(barrier, len(around))

    def span(step, unit, extent, sending):
        if step == 0:
            return pl.ds(unit, extent)
        if sending:
            return pl.ds(unit if step < 0 else extent, unit)
        return pl.ds(unit + extent if step < 0 else 0, unit)

    copies = []
    for index, (a, b) in enumerate(around):
        copy = pltpu.make_async_remote_copy(
            src_ref=field.at[:, span(a, SUB, height, True), span(b, LANES, width, True)],
            dst_ref=field.at[:, span(a, SUB, height, False), span(b, LANES, width, False)],
            send_sem=send.at[index], recv_sem=recv.at[index],
            device_id=device(a, b), device_id_type=MESH,
        )
        copy.start()
        copies.append(copy)
    for copy in copies:
        copy.wait()
    flood_steps(n_row, n_col, height, width, field, depth_out, one_out, two_out)


def face_flux(surface, after, bed, bed_after, old):
    depth = jnp.maximum(jnp.maximum(surface, after) - jnp.maximum(bed, bed_after), DEPTH_FLOOR)
    pushed = old - (GRAVITY * TIME_STEP / CELL_WIDTH) * depth * (after - surface)
    drag = jnp.exp(jnp.log(depth) * (-7.0 / 3.0))
    return pushed / (1.0 + (GRAVITY * TIME_STEP * MANNING_SQ) * jnp.abs(old) * drag)


def flood_steps(n_row, n_col, height, width, field, depth_out, one_out, two_out):
    my_row, my_col = lax.axis_index("row"), lax.axis_index("col")
    depth, bed, one, two, mask = [field[q] for q in range(5)]
    tall, broad = depth.shape
    rows = lax.broadcasted_iota(i32, (tall, broad), 0)
    cols = lax.broadcasted_iota(i32, (tall, broad), 1)
    shut_one = ((rows == SUB - 1) & (my_row == 0)) | (
        (rows == SUB + height - 1) & (my_row == n_row - 1)
    )
    shut_two = ((cols == LANES - 1) & (my_col == 0)) | (
        (cols == LANES + width - 1) & (my_col == n_col - 1)
    )
    weight = mask * (TIME_STEP / CELL_WIDTH)
    below = lambda x: pltpu.roll(x, tall - 1, 0)
    above = lambda x: pltpu.roll(x, 1, 0)
    after = lambda x: pltpu.roll(x, broad - 1, 1)
    before = lambda x: pltpu.roll(x, 1, 1)
    bed_below, bed_after = below(bed), after(bed)
    for repeat in range(2):
        surface = bed + depth
        one = face_flux(surface, below(surface), bed, bed_below, one)
        one = jnp.where(shut_one, 0.0, one)
        two = face_flux(surface, after(surface), bed, bed_after, two)
        two = jnp.where(shut_two, 0.0, two)
        depth = depth + weight * ((above(one) - one) + (before(two) - two))
    inner = (slice(SUB, SUB + height), slice(LANES, LANES + width))
    depth_out[...] = depth[inner]
    one_out[...] = one[inner]
    two_out[...] = two[inner]


def flood(depth, bed, one, two, mask, n_row, n_col):
    height, width = depth.shape
    dma = pltpu.SemaphoreType.DMA((8,))
    return pl.pallas_call(
        functools.partial(flood_kernel, n_row, n_col, height, width),
        out_shape=(jax.ShapeDtypeStruct(depth.shape, f32),) * 3,
        in_specs=[VMEM_SPEC] * 5,
        out_specs=(VMEM_SPEC,) * 3,
        scratch_shapes=[
            pltpu.VMEM((5, height + 2 * SUB, width + 2 * LANES), f32), dma, dma,
        ],
        compiler_params=pltpu.CompilerParams(collective_id=1, has_side_effects=True),
        name="flood",
    )(depth, bed, one, two, mask)


def local_step(
    river_lower, river_main, river_upper, river_rhs, weir_crest, weir_regime, weir_tile,
    weir_row, weir_col, bed_level, water_depth, flux_first, flux_second, wet_mask,
):
    n_row, n_col = lax.axis_size("row"), lax.axis_size("col")
    devices = n_row * n_col
    state, keep, slope = solve_river(
        river_lower, river_main, river_upper, river_rhs, weir_crest, weir_regime, n_row
    )
    tile = weir_tile.reshape(-1, LANES)
    capacity = 2 * weir_row.size // devices
    outgoing = fill_slots(tile, weir_row, weir_col, keep, slope, devices, capacity)
    arrived = lax.all_to_all(outgoing, ("row", "col"), split_axis=1, concat_axis=1, tiled=True)
    wetted = apply_weirs(arrived, bed_level, water_depth)
    depth, one, two = flood(wetted, bed_level, flux_first, flux_second, wet_mask, n_row, n_col)
    return (state, depth, one, two)


def solution(mesh):
    tile2 = P("row", "col")
    block = P("row", None, None, "col")
    in_specs = (
        block, block, block, P("row", None, "col"), tile2, tile2,
        P("row", "col", None, None, None), tile2, tile2, tile2, tile2, tile2, tile2, tile2,
    )
    out_specs = (P("row", None, "col"), tile2, tile2, tile2)
    return jax.shard_map(
        local_step, mesh=mesh, in_specs=in_specs, out_specs=out_specs, check_vma=False
    )
```

profile of v0, /device:TPU:1, one launch (start us, length us, event | category | flops | bytes accessed | tf_op | source)
XLA Modules:
  0.0 79.7 jit_solution(13157018104859182043)
XLA Ops:
  0.6 13.9 %river.1 = (f32[16,16,128]{2,1,0:T(8,128)}, f32[16,8,128]{2,1,0:T(8,128)}, f32[16,8,128]{2,1,0:T(8,128)}) custom-call(f32[16,2,16,128]{3,2,1,0:T(8,128)} %bitcast.28, f32[16,2,16,128]{3,2,1,0:T(8,128)} %bitcast.29, f32[16,2,16,128]{3,2,1,0:T(8,128)} %bitcast.30, f32[16,16,128]{2,1,0:T(8,128)} %bitcast.32, f32[16,1024]{1,0:T(8,128)} %crest_ref.1, ...), custom_call_target="tpu_custom_call" | custom-call | tf_op jit(solution)/shard_map/river/pallas_call | solution.py:209
  14.6 15.6 %fill.1 = f32[3,128,256]{2,1,0:T(8,128)} custom-call(s32[128,128]{1,0:T(8,128)} %bitcast.33, s32[16,1024]{1,0:T(8,128)} %row_ref.1, s32[16,1024]{1,0:T(8,128)} %col_ref.1, f32[128,128]{1,0:T(8,128)} %bitcast.34, f32[128,128]{1,0:T(8,128)} %bitcast.35), custom_call_target="tpu_custom_call" | custom-call | tf_op jit(solution)/shard_map/fill/pallas_call | solution.py:301
  30.1 2.1 %copy.28 = f32[3,128,256]{2,0,1:T(4,128)} copy(f32[3,128,256]{2,1,0:T(8,128)} %fill.1) | data formatting | bytes 786432 | tf_op jit(solution)/shard_map/fill/pallas_call | solution.py:301
  32.2 8.5 %all-to-all-start = ((f32[3,128,256]{2,0,1:T(4,128)}), f32[3,128,256]{2,0,1:T(4,128)S(1)}, u32[]{:S(2)}, u32[]{:S(2)}) async-start(f32[3,128,256]{2,0,1:T(4,128)} %copy.28), calls=%async_computation | async-start | bytes 1048576 | tf_op jit(solution)/shard_map/all_to_all | solution.py:479
  40.7 13.4 %all-to-all-done = f32[3,128,256]{2,0,1:T(4,128)S(1)} async-done(((f32[3,128,256]{2,0,1:T(4,128)}), f32[3,128,256]{2,0,1:T(4,128)S(1)}, u32[]{:S(2)}, u32[]{:S(2)}) %all-to-all-start) | async-done | bytes 393248 | tf_op jit(solution)/shard_map/all_to_all | solution.py:479
  54.1 0.8 %copy.29.in_ref = f32[3,128,256]{2,1,0:T(8,128)} copy(f32[3,128,256]{2,0,1:T(4,128)S(1)} %all-to-all-done) | data formatting | bytes 786432 | tf_op jit(solution)/shard_map/all_to_all | solution.py:479
  54.9 9.4 %apply.1.depth_ref = f32[32,512]{1,0:T(8,128)} custom-call(f32[3,128,256]{2,1,0:T(8,128)} %copy.29.in_ref, f32[32,512]{1,0:T(8,128)} %bed_ref.3, f32[32,512]{1,0:T(8,128)} %depth_ref.1), custom_call_target="tpu_custom_call" | custom-call | tf_op jit(solution)/shard_map/apply/pallas_call | solution.py:359
  64.3 0.0 copy-start
  64.3 12.2 %flood.1 = (f32[32,512]{1,0:T(8,128)}, f32[32,512]{1,0:T(8,128)}, f32[32,512]{1,0:T(8,128)}) custom-call(f32[32,512]{1,0:T(8,128)} %apply.1.depth_ref, f32[32,512]{1,0:T(8,128)} %bed_ref.3, f32[32,512]{1,0:T(8,128)} %one_ref.1, f32[32,512]{1,0:T(8,128)} %two_ref.1, s32[32,512]{1,0:T(8,128)} %mask_ref.1), custom_call_target="tpu_custom_call" | custom-call | tf_op jit(solution)/shard_map/flood/pallas_call | solution.py:454
  76.5 0.0 copy-done
  76.5 0.0 copy-start.3
  76.5 0.7 copy.34
  77.2 0.2 copy-done.3
  77.4 0.0 copy-start.2
  77.4 0.6 copy.35
  78.0 0.2 copy-done.2
  78.2 0.0 copy-start.1
  78.2 0.6 copy.36
  78.9 0.2 copy-done.1
  79.1 0.6 copy.37
Async XLA Ops:
  32.2 21.9 %all-to-all-start = ((f32[3,128,256]{2,0,1:T(4,128)}), f32[3,128,256]{2,0,1:T(4,128)S(1)}, u32[]{:S(2)}, u32[]{:S(2)}) async-start(f32[3,128,256]{2,0,1:T(4,128)} %copy.28), calls=%async_computation | async-start | bytes 1048576 | tf_op jit(solution)/shard_map/all_to_all | solution.py:479
  64.3 12.2 %copy-start = (f32[16,16,128]{2,1,0:T(8,128)S(1)}, f32[16,16,128]{2,1,0:T(8,128)}, u32[]{:S(2)}) copy-start(f32[16,16,128]{2,1,0:T(8,128)} %get-tuple-element.10) | copy-start | bytes 393220
  76.5 0.8 %copy-start.3 = (f32[32,512]{1,0:T(8,128)S(1)}, f32[32,512]{1,0:T(8,128)}, u32[]{:S(2)}) copy-start(f32[32,512]{1,0:T(8,128)} %get-tuple-element.21) | copy-start | bytes 196612
  77.4 0.9 %copy-start.2 = (f32[32,512]{1,0:T(8,128)S(1)}, f32[32,512]{1,0:T(8,128)}, u32[]{:S(2)}) copy-start(f32[32,512]{1,0:T(8,128)} %get-tuple-element.22) | copy-start | bytes 196612
  78.2 0.9 %copy-start.1 = (f32[32,512]{1,0:T(8,128)S(1)}, f32[32,512]{1,0:T(8,128)}, u32[]{:S(2)}) copy-start(f32[32,512]{1,0:T(8,128)} %get-tuple-element.23) | copy-start | bytes 196612
where the time goes:
time: 80.2 us; the launch traced here: 79.7 us
  Pallas kernels  51.1 us (64%)
  waiting for transfers between devices  13.4 us (17%)
  starting transfers between devices  8.48 us (11%)
  local copies, waits for them, and re-layouts  6.06 us (8%)
    pallas_call x1, Pallas kernels, fill_slots(): pl.pallas_call(functools.partial(fill_kernel, devices, capacity), out_sha...  15.6 us
    pallas_call x1, Pallas kernels, solve_river(): pl.pallas_call(functools.partial(river_kernel, n_row, sections), out_shap...  13.9 us
    all_to_all x1, waiting for transfers between devices, local_step(): lax.all_to_all(outgoing, ('row', 'col'), split_axis=1, concat_axis=1, til...  13.4 us
    pallas_call x1, Pallas kernels, flood(): pl.pallas_call(functools.partial(flood_kernel, n_row, n_col, height, widt...  12.2 us
    pallas_call x1, Pallas kernels, apply_weirs(): pl.pallas_call(apply_kernel, out_shape=jax.ShapeDtypeStruct(depth.shape,...  9.42 us
    all_to_all x1, starting transfers between devices, local_step(): lax.all_to_all(outgoing, ('row', 'col'), split_axis=1, concat_axis=1, til...  8.48 us
    unnamed x12, local copies, waits for them, and re-layouts  3.19 us
    pallas_call x1, local copies, waits for them, and re-layouts, fill_slots(): pl.pallas_call(functools.partial(fill_kernel, devices, capacity), out_sha...  2.06 us
  transfers between devices with their start and end apart: 1, of which 1 were waited for; matrix products, arithmetic and copies ran while one was open for 0% of the time, Pallas kernels for 0%

commit v1 on v0

v1 whole, which is shorter than its diff:
```python
import functools

import jax
import jax.numpy as jnp
from jax import lax
from jax.experimental import pallas as pl
from jax.experimental.pallas import tpu as pltpu
from jax.sharding import PartitionSpec as P

GRAVITY = 9.81
TIME_STEP = 1.0
CELL_WIDTH = 10.0
MANNING_SQ = 0.0009
DEPTH_FLOOR = 0.05
WEIR_GAIN = 0.5
FREE_COEF = 0.5
SUB_COEF = 0.4
SUB_OFFSET = 0.25
GATE_COEF = 0.2
LANES = 128
SUB = 8
MESH = pl.DeviceIdType.MESH
VMEM_SPEC = pl.BlockSpec(memory_space=pltpu.VMEM)
f32 = jnp.float32
bf16 = jnp.bfloat16
i32 = jnp.int32


def mat_mat(a, b):
    return [
        a[0] * b[0] + a[1] * b[2],
        a[0] * b[1] + a[1] * b[3],
        a[2] * b[0] + a[3] * b[2],
        a[2] * b[1] + a[3] * b[3],
    ]


def mat_vec(a, v):
    return [a[0] * v[0] + a[1] * v[1], a[2] * v[0] + a[3] * v[1]]


def minus(a, b):
    return [x - y for x, y in zip(a, b)]


def plus(a, b):
    return [x + y for x, y in zip(a, b)]


def negative(a):
    return [-x for x in a]


def inverse(m):
    scale = 1.0 / (m[0] * m[3] - m[1] * m[2])
    return [m[3] * scale, -(m[1] * scale), -(m[2] * scale), m[0] * scale]


CHUNK = 1024
HALF = 64


def split_two(x):
    high = x.astype(bf16).astype(f32)
    return high, x - high


def both(x, row):
    return jnp.concatenate([x[row : row + 1, :], x[row + 1 : row + 2, :]], axis=1)


def nt_dot(left, right):
    return lax.dot_general(left, right, (((1,), (1,)), ((), ())), preferred_element_type=f32)


def solve_local(sections, lower_ref, main_ref, upper_ref, rhs_ref, couple, local, heads):
    def block(ref, s):
        return [ref[s, i, pl.ds(j, SUB, stride=2), :] for i in range(2) for j in range(2)]

    coupled = value = spike = None
    for s in range(sections):
        low, main, up = block(lower_ref, s), block(main_ref, s), block(upper_ref, s)
        right = [rhs_ref[s, pl.ds(j, SUB, stride=2), :] for j in range(2)]
        if s == 0:
            inv = inverse(main)
            value = mat_vec(inv, right)
            spike = negative(mat_mat(inv, low))
        else:
            inv = inverse(minus(main, mat_mat(low, coupled)))
            value = mat_vec(inv, minus(right, mat_vec(low, value)))
            spike = negative(mat_mat(inv, mat_mat(low, spike)))
        coupled = mat_mat(inv, up)
        for q in range(4):
            couple[s, q] = coupled[q]
            local[s, 2 + q] = spike[q]
        for q in range(2):
            local[s, q] = value[q]
    after = negative(coupled)
    for q in range(4):
        local[sections - 1, 6 + q] = after[q]
    tail = value + spike + after
    for s in range(sections - 2, -1, -1):
        here = [couple[s, q] for q in range(4)]
        value = minus([local[s, q] for q in range(2)], mat_vec(here, value))
        spike = minus([local[s, 2 + q] for q in range(4)], mat_mat(here, spike))
        after = negative(mat_mat(here, after))
        for q in range(2):
            local[s, q] = value[q]
        for q in range(4):
            local[s, 2 + q] = spike[q]
            local[s, 6 + q] = after[q]
    for q, face in enumerate(value + spike + after + tail):
        heads[:, q, :] = face


def solve_reduced(n_row, head_in, edges):
    zero = jnp.zeros((1, LANES), f32)
    one = jnp.ones((1, LANES), f32)
    prev_couple, prev_value = [zero] * 4, [zero] * 2
    done = []
    for p in range(n_row):
        part = [head_in[p, q : q + 1, :] for q in range(20)]
        head_y, head_l, head_r = part[0:2], part[2:6], part[6:10]
        tail_y, tail_l, tail_r = part[10:12], part[12:16], part[16:20]
        inv = inverse(plus([one, zero, zero, one], mat_mat(head_l, prev_couple)))
        first_couple = negative(mat_mat(inv, head_r))
        first_value = mat_vec(inv, plus(head_y, mat_vec(head_l, prev_value)))
        bridge = mat_mat(tail_l, prev_couple)
        last_couple = minus(negative(tail_r), mat_mat(bridge, first_couple))
        last_value = minus(plus(tail_y, mat_vec(tail_l, prev_value)), mat_vec(bridge, first_value))
        done.append((first_couple, first_value, last_couple, last_value))
        prev_couple, prev_value = last_couple, last_value
    following = [zero] * 2
    for p in range(n_row - 1, -1, -1):
        first_couple, first_value, last_couple, last_value = done[p]
        for q in range(2):
            edges[p, 2 + q : 3 + q, :] = following[q]
        last = minus(last_value, mat_vec(last_couple, following))
        if p + 1 < n_row:
            for q in range(2):
                edges[p + 1, q : q + 1, :] = last[q]
        following = minus(first_value, mat_vec(first_couple, following))
    for q in range(2):
        edges[0, q : q + 1, :] = zero


def step_kernel(
    n_row, n_col,
    lower_ref, main_ref, upper_ref, rhs_ref, crest_ref, regime_ref, tile_ref, row_ref, col_ref,
    bed_ref, depth_ref, one_ref, two_ref, mask_ref,
    state_ref, field,
    couple, local, heads, head_in, edges, edge_in, crest, regime, cells, tiles, earlier,
    hot, ranks, left, total, pieces, slots, land, one_hot, two_hot, scatter,
    ready, send_one, recv_one, send_two, recv_two, send_all, recv_all,
    send_fix, recv_fix, send_wet, recv_wet,
):
    sections = rhs_ref.shape[0]
    height, width = bed_ref.shape
    devices = n_row * n_col
    capacity = ranks.shape[1]
    chunks = hot.shape[0]
    my_row, my_col = lax.axis_index("row"), lax.axis_index("col")
    me = my_row * n_col + my_col
    barrier = pltpu.get_barrier_semaphore()
    col_peers = [(my_row, lax.rem(my_col + k, n_col)) for k in range(1, n_col)]
    row_peers = [lax.rem(my_row + k, n_row) for k in range(1, n_row)]
    for p in row_peers:
        pl.semaphore_signal(barrier, inc=1, device_id=(p, my_col), device_id_type=MESH)
    for device in col_peers:
        pl.semaphore_signal(barrier, inc=1, device_id=device, device_id_type=MESH)

    solve_local(sections, lower_ref, main_ref, upper_ref, rhs_ref, couple, local, heads)

    pl.semaphore_wait(barrier, n_row + n_col - 2)

    def exchange(source, target, send, recv):
        copies = []
        for k, p in enumerate(row_peers):
            copy = pltpu.make_async_remote_copy(
                src_ref=source.at[p], dst_ref=target.at[my_row],
                send_sem=send.at[k], recv_sem=recv.at[k],
                device_id=(p, my_col), device_id_type=MESH,
            )
            copy.start()
            copies.append(copy)
        target[my_row] = source[my_row]
        return copies

    copies = exchange(heads, head_in, send_one, recv_one)
    for device in col_peers:
        pl.semaphore_signal(ready, inc=1, device_id=device, device_id_type=MESH)

    for half in range(sections // SUB):
        for k in range(SUB):
            rows, cols = pl.ds(half * SUB, SUB), pl.ds(k * LANES, LANES)
            crest[rows, k, :] = crest_ref[rows, cols]
            regime[rows, k, :] = regime_ref[rows, cols]
            col = col_ref[rows, cols]
            cells[0, rows, k, :] = (row_ref[rows, cols] + (col >> 8) * height).astype(f32)
            cells[1, rows, k, :] = (col & 255).astype(f32)
    tiles[...] = (tile_ref[...] - me + devices) & (devices - 1)
    wide = 2 * LANES
    earlier[...] = (
        lax.broadcasted_iota(i32, (wide, wide), 0) < lax.broadcasted_iota(i32, (wide, wide), 1)
    ).astype(f32).astype(bf16)
    every = jnp.ones((wide, LANES), bf16)
    tile_table = lax.broadcasted_iota(i32, (devices, wide), 0)
    rank_table = lax.broadcasted_iota(i32, (capacity, wide), 0).astype(f32)

    def rank_step(index, offset):
        here = tiles[pl.ds(pl.multiple_of(index * SUB, SUB), SUB), :]
        for part in range(CHUNK // wide):
            lanes = pl.ds(part * wide, wide)
            mine = both(here, 2 * part) == tile_table
            mine_one = jnp.where(mine, 1.0, 0.0).astype(bf16)
            hot[index, :, lanes] = mine_one
            within = jnp.dot(mine_one, earlier[...], preferred_element_type=f32)
            counts = jnp.dot(mine_one, every, preferred_element_type=f32)
            base = within + jnp.concatenate([offset, offset], axis=1)
            rank = jnp.sum(jnp.where(mine, base, 0.0), axis=0, keepdims=True)
            offset = offset + counts
            ranks[index, :, lanes] = jnp.where(rank == rank_table, 1.0, 0.0).astype(bf16)
        return offset

    lax.fori_loop(0, chunks, rank_step, jnp.zeros((devices, LANES), f32))
    for copy in copies:
        copy.wait()

    solve_reduced(n_row, head_in, edges)
    copies = exchange(edges, edge_in, send_two, recv_two)

    inner = (pl.ds(SUB, height), pl.ds(LANES, width))
    for q, ref in enumerate((bed_ref, one_ref, two_ref)):
        field[(1 + q,) + inner] = ref[...]
    field[(4,) + inner] = mask_ref[...].astype(f32)

    def fill(index, values, offsets, extent):
        for part in range(CHUNK // wide):
            lanes = pl.ds(part * wide, wide)
            mine = hot[index, offsets, lanes]
            for q, value in enumerate(values):
                row = jnp.broadcast_to(both(value, 2 * part), (extent, wide)).astype(bf16)
                left[pl.ds(q * extent, extent), lanes] = mine * row
        total[...] += nt_dot(left[...], ranks[index])

    def put(slot, offsets, value):
        slots[offsets, slot, :] = value[:, :LANES]
        slots[offsets, slot + 1, :] = value[:, LANES:]

    total[...] = jnp.zeros_like(total)

    def cell_step(index, carry):
        fill(index, [cells[0, index], cells[1, index]], pl.ds(0, devices), devices)
        return carry

    lax.fori_loop(0, chunks, cell_step, 0)
    put(4, pl.ds(0, devices), total[pl.ds(0, devices), :] * 256.0 + total[pl.ds(devices, devices), :])
    pl.semaphore_wait(ready, n_col - 1)
    for copy in copies:
        copy.wait()

    around = [(a, b) for a in (-1, 0, 1) for b in (-1, 0, 1) if (a, b) != (0, 0)]

    def span(step, unit, extent, sending):
        if step == 0:
            return pl.ds(unit, extent)
        if sending:
            return pl.ds(unit if step < 0 else extent, unit)
        return pl.ds(unit + extent if step < 0 else 0, unit)

    def halo(fields, send, recv):
        sent = []
        for index, (a, b) in enumerate(around):
            copy = pltpu.make_async_remote_copy(
                src_ref=field.at[fields, span(a, SUB, height, True), span(b, LANES, width, True)],
                dst_ref=field.at[fields, span(a, SUB, height, False), span(b, LANES, width, False)],
                send_sem=send.at[index], recv_sem=recv.at[index],
                device_id=(lax.rem(my_row + a + n_row, n_row), lax.rem(my_col + b + n_col, n_col)),
                device_id_type=MESH,
            )
            copy.start()
            sent.append(copy)
        return sent

    fixed = halo(pl.ds(1, 4), send_fix, recv_fix)

    before = [edge_in[:, q, :] for q in range(2)]
    behind = [edge_in[:, 2 + q, :] for q in range(2)]
    for s in range(sections):
        solved = [local[s, q] for q in range(2)]
        solved = plus(solved, mat_vec([local[s, 2 + q] for q in range(4)], before))
        solved = plus(solved, mat_vec([local[s, 6 + q] for q in range(4)], behind))
        for j in range(2):
            state_ref[s, pl.ds(j, SUB, stride=2), :] = solved[j]
        phase = solved[0]
        head = jnp.maximum(phase - crest[s], 0.0)
        kind = regime[s]
        free = jnp.where(kind == 0, FREE_COEF * head * jnp.sqrt(head), 0.0)
        slope = jnp.where(
            kind == 1,
            SUB_COEF * jnp.sqrt(head + SUB_OFFSET),
            jnp.where(kind == 2, GATE_COEF, 0.0),
        )
        keep = split_two(WEIR_GAIN * (free + slope * phase))
        slope = split_two(WEIR_GAIN * slope)
        for q, piece in enumerate(keep + slope):
            pieces[q, s] = piece

    def send_slot(k):
        peer = lax.rem(me + k, devices)
        return pltpu.make_async_remote_copy(
            src_ref=slots.at[k], dst_ref=land.at[k],
            send_sem=send_all.at[k // SUB], recv_sem=recv_all.at[k // SUB],
            device_id=(peer // n_col, lax.rem(peer, n_col)), device_id_type=MESH,
        )

    per_step = HALF // chunks
    for side in range(devices // HALF):
        offsets = pl.ds(side * HALF, HALF)
        total[...] = jnp.zeros_like(total)

        def value_step(index, carry):
            if side > 0:
                for j in range(per_step):
                    k = (side - 1) * HALF + index * per_step + j
                    if j == 0 and side == 1:
                        @pl.when(index > 0)
                        def _():
                            send_slot(k).start()
                    else:
                        send_slot(k).start()
            fill(index, [pieces[q, index] for q in range(4)], offsets, HALF)
            return carry

        lax.fori_loop(0, chunks, value_step, 0)
        piece = lambda q: total[pl.ds(q * HALF, HALF), :]
        put(0, offsets, piece(0) + piece(1))
        put(2, offsets, piece(2) + piece(3))
    land[0] = slots[0]

    cells_one, cells_two = 2 * height, 256
    scatter[...] = jnp.zeros_like(scatter)
    one_table = lax.broadcasted_iota(i32, (cells_one, capacity), 0).astype(f32)
    two_table = lax.broadcasted_iota(i32, (cells_two, capacity), 0).astype(f32)

    def arrive(first, count, group):
        pltpu.make_async_remote_copy(
            src_ref=slots.at[pl.ds(first, count)], dst_ref=land.at[pl.ds(first, count)],
            send_sem=send_all.at[group], recv_sem=recv_all.at[group],
            device_id=(my_row, my_col), device_id_type=MESH,
        ).wait_recv()

    def apply_step(index):
        first_slot = pl.multiple_of(index * SUB, SUB)
        here = [land[pl.ds(first_slot, SUB), q, :] for q in range(6)]
        cell = here[4:]
        first = [jnp.floor(c * (1.0 / 256.0)) for c in cell]
        second = [c - f * 256.0 for c, f in zip(cell, first)]
        keep = [split_two(x) for x in here[0:2]]
        slope = [split_two(x) for x in here[2:4]]
        values = [[v[q] for v in pair] for pair in (keep, slope) for q in range(2)]
        for part in range(SUB):
            row = lambda v: jnp.concatenate([x[part : part + 1, :] for x in v], axis=1)
            lanes = pl.ds(part * capacity, capacity)
            two_hot[:, lanes] = jnp.where(row(second) == two_table, 1.0, 0.0).astype(bf16)
            mine = jnp.where(row(first) == one_table, 1.0, 0.0).astype(bf16)
            for q in range(4):
                value = jnp.broadcast_to(row(values[q]), (cells_one, capacity)).astype(bf16)
                one_hot[pl.ds(q * cells_one, cells_one), lanes] = mine * value
        scatter[...] += nt_dot(one_hot[...], two_hot[...])

    groups = devices // SUB
    def early_step(index, carry):
        for j in range(SUB):
            send_slot(devices - HALF + index * SUB + j).start()
        @pl.when(index == 0)
        def _():
            arrive(1, SUB - 1, 0)
        @pl.when(index > 0)
        def _():
            arrive(index * SUB, SUB, index)
        apply_step(index)
        return carry

    lax.fori_loop(0, HALF // SUB, early_step, 0)

    def late_step(index, carry):
        arrive(index * SUB, SUB, index)
        apply_step(index)
        return carry

    lax.fori_loop(HALF // SUB, groups, late_step, 0)

    piece = lambda q, side: scatter[pl.ds(q * cells_one + side * height, height), :]
    for side in range(2):
        cols = pl.ds(side * cells_two, cells_two)
        keep = piece(0, side) + piece(1, side)
        slope = piece(2, side) + piece(3, side)
        depth = depth_ref[:, cols]
        surface = bed_ref[:, cols] + depth
        field[0, pl.ds(SUB, height), pl.ds(LANES + side * cells_two, cells_two)] = jnp.maximum(
            depth + (keep - slope * surface), 0.0
        )
    wet = halo(pl.ds(0, 1), send_wet, recv_wet)

    def sent(first, count, group):
        pltpu.make_async_remote_copy(
            src_ref=slots.at[pl.ds(first, count)], dst_ref=land.at[pl.ds(first, count)],
            send_sem=send_all.at[group], recv_sem=recv_all.at[group],
            device_id=(my_row, my_col), device_id_type=MESH,
        ).wait_send()

    sent(1, SUB - 1, 0)

    def sent_step(index, carry):
        sent(index * SUB, SUB, index)
        return carry

    lax.fori_loop(1, groups, sent_step, 0)
    for copy in fixed + wet:
        copy.wait()


def dense(x):
    x = x.reshape(x.shape[:-1] + (SUB, LANES))
    x = jnp.swapaxes(x, -2, -3)
    return x.reshape(x.shape[:-3] + (2 * SUB, LANES))


def whole_step(args, n_row, n_col):
    lower, main, upper, rhs, crest, regime, tile, row, col, bed, depth, one, two, mask = args
    sections = rhs.shape[0]
    height, width = bed.shape
    devices = n_row * n_col
    capacity = 2 * row.size // devices
    chunks = row.size // CHUNK
    wide = lambda *lead: pltpu.VMEM(lead + (SUB, LANES), f32)
    vmem = lambda *shape: pltpu.VMEM(shape, f32)
    half = lambda *shape: pltpu.VMEM(shape, bf16)
    dma = lambda n: pltpu.SemaphoreType.DMA((n,))
    return pl.pallas_call(
        functools.partial(step_kernel, n_row, n_col),
        out_shape=(
            jax.ShapeDtypeStruct((sections, 2 * SUB, LANES), f32),
            jax.ShapeDtypeStruct((5, height + 2 * SUB, width + 2 * LANES), f32),
        ),
        in_specs=[VMEM_SPEC] * 14,
        out_specs=(VMEM_SPEC,) * 2,
        scratch_shapes=[
            wide(sections, 4), wide(sections, 10),
            vmem(n_row, 24, LANES), vmem(n_row, 24, LANES), wide(n_row), wide(n_row),
            wide(sections), pltpu.VMEM((sections, SUB, LANES), i32), wide(2, sections),
            pltpu.VMEM((row.size // LANES, LANES), i32), half(2 * LANES, 2 * LANES),
            half(chunks, devices, CHUNK), half(chunks, capacity, CHUNK),
            half(4 * HALF, CHUNK), vmem(4 * HALF, capacity), wide(4, sections),
            vmem(devices, 6, LANES), vmem(devices, 6, LANES),
            half(8 * height, SUB * capacity), half(256, SUB * capacity), vmem(8 * height, 256),
            pltpu.SemaphoreType.REGULAR,
            dma(n_row - 1), dma(n_row - 1), dma(n_row - 1), dma(n_row - 1),
            dma(devices // SUB), dma(devices // SUB), dma(8), dma(8), dma(8), dma(8),
        ],
        compiler_params=pltpu.CompilerParams(
            collective_id=0, has_side_effects=True, vmem_limit_bytes=40 << 20
        ),
        name="step",
    )(
        dense(lower), dense(main), dense(upper), dense(rhs), crest, regime,
        tile.reshape(-1, LANES), row, col, bed, depth, one, two, mask,
    )


def face_flux(surface, after, bed, bed_after, old):
    depth = jnp.maximum(jnp.maximum(surface, after) - jnp.maximum(bed, bed_after), DEPTH_FLOOR)
    pushed = old - (GRAVITY * TIME_STEP / CELL_WIDTH) * depth * (after - surface)
    drag = jnp.exp(jnp.log(depth) * (-7.0 / 3.0))
    return pushed / (1.0 + (GRAVITY * TIME_STEP * MANNING_SQ) * jnp.abs(old) * drag)


def flood_kernel(n_row, n_col, field, state_ref, depth_out, one_out, two_out, state_out, sem):
    copy = pltpu.make_async_copy(state_ref, state_out, sem)
    copy.start()
    height, width = depth_out.shape
    my_row, my_col = lax.axis_index("row"), lax.axis_index("col")
    depth, bed, one, two, mask = [field[q] for q in range(5)]
    tall, broad = depth.shape
    rows = lax.broadcasted_iota(i32, (tall, broad), 0)
    cols = lax.broadcasted_iota(i32, (tall, broad), 1)
    shut_one = ((rows == SUB - 1) & (my_row == 0)) | (
        (rows == SUB + height - 1) & (my_row == n_row - 1)
    )
    shut_two = ((cols == LANES - 1) & (my_col == 0)) | (
        (cols == LANES + width - 1) & (my_col == n_col - 1)
    )
    weight = mask * (TIME_STEP / CELL_WIDTH)
    below = lambda x: pltpu.roll(x, tall - 1, 0)
    above = lambda x: pltpu.roll(x, 1, 0)
    after = lambda x: pltpu.roll(x, broad - 1, 1)
    before = lambda x: pltpu.roll(x, 1, 1)
    bed_below, bed_after = below(bed), after(bed)
    for repeat in range(2):
        surface = bed + depth
        one = face_flux(surface, below(surface), bed, bed_below, one)
        one = jnp.where(shut_one, 0.0, one)
        two = face_flux(surface, after(surface), bed, bed_after, two)
        two = jnp.where(shut_two, 0.0, two)
        depth = depth + weight * ((above(one) - one) + (before(two) - two))
    inner = (slice(SUB, SUB + height), slice(LANES, LANES + width))
    depth_out[...] = depth[inner]
    one_out[...] = one[inner]
    two_out[...] = two[inner]
    copy.wait()


def flood(field, state, shape, n_row, n_col):
    return pl.pallas_call(
        functools.partial(flood_kernel, n_row, n_col),
        out_shape=(jax.ShapeDtypeStruct(shape, f32),) * 3
        + (jax.ShapeDtypeStruct(state.shape, f32),),
        in_specs=[VMEM_SPEC, pl.BlockSpec(memory_space=pl.ANY)],
        out_specs=(VMEM_SPEC,) * 3 + (pl.BlockSpec(memory_space=pl.ANY),),
        scratch_shapes=[pltpu.SemaphoreType.DMA],
        name="flood",
    )(field, state)


def local_step(*args):
    n_row, n_col = lax.axis_size("row"), lax.axis_size("col")
    rhs, bed = args[3], args[9]
    state, field = whole_step(args, n_row, n_col)
    depth, one, two, state = flood(field, state, bed.shape, n_row, n_col)
    state = jnp.swapaxes(state.reshape(-1, SUB, 2, LANES), 1, 2).reshape(rhs.shape)
    return (state, depth, one, two)


def solution(mesh):
    tile2 = P("row", "col")
    block = P("row", None, None, "col")
    in_specs = (
        block, block, block, P("row", None, "col"), tile2, tile2,
        P("row", "col", None, None, None), tile2, tile2, tile2, tile2, tile2, tile2, tile2,
    )
    out_specs = (P("row", None, "col"), tile2, tile2, tile2)
    return jax.shard_map(
        local_step, mesh=mesh, in_specs=in_specs, out_specs=out_specs, check_vma=False
    )
```

time: 80.2 us -> 72.1 us (0.90)
  waiting for transfers between devices: 13.4 us -> 0 us
  starting transfers between devices: 8.48 us -> 0 us
  local copies, waits for them, and re-layouts: 6.06 us -> 13.7 us
  Pallas kernels: 51.1 us -> 57 us
    all_to_all x1 -> x0, waiting for transfers between devices: 13.4 us -> none  [local_step(): lax.all_to_all(outgoing, ('row', 'col'), split_axis=1, concat_axis=1, til...]
    unnamed x12 -> x32, local copies, waits for them, and re-layouts: 3.19 us -> 13.7 us
    all_to_all x1 -> x0, starting transfers between devices: 8.48 us -> none  [local_step(): lax.all_to_all(outgoing, ('row', 'col'), split_axis=1, concat_axis=1, til...]
    pallas_call x4 -> x2, Pallas kernels: 51.1 us -> 57 us  [the longest x1 50.1 us: whole_step(): pl.pallas_call(functools.partial(step_kernel, n_row, n_col), out_shape=(j...]
    pallas_call x1 -> x0, local copies, waits for them, and re-layouts: 2.06 us -> none  [fill_slots(): pl.pallas_call(functools.partial(fill_kernel, devices, capacity), out_sha...]
    all_to_all x1 -> x0, local copies, waits for them, and re-layouts: 0.82 us -> none  [local_step(): lax.all_to_all(outgoing, ('row', 'col'), split_axis=1, concat_axis=1, til...]
  transfers between devices with their start and end apart: 1 -> 0, of which waited for: 1 -> 0; matrix products, arithmetic and copies ran while one was open for 0% -> 0% of each run, Pallas kernels for 0% -> 0%
where the time goes in v1:
time: 72.1 us; the launch traced here: 71.3 us
  Pallas kernels  57 us (79%)
  local copies, waits for them, and re-layouts  13.7 us (19%)
    pallas_call x1, Pallas kernels, whole_step(): pl.pallas_call(functools.partial(step_kernel, n_row, n_col), out_shape=(j...  50.1 us
    unnamed x32, local copies, waits for them, and re-layouts  13.7 us
    pallas_call x1, Pallas kernels, flood(): pl.pallas_call(functools.partial(flood_kernel, n_row, n_col), out_shape=(...  6.87 us

profile of v1, /device:TPU:1, one launch (start us, length us, event | category | flops | bytes accessed | tf_op | source)
XLA Modules:
  0.0 71.3 jit_solution(5712472869522084397)
XLA Ops:
  0.6 0.0 copy-start.1
  0.6 0.9 %copy-done.1 = f32[16,2,2,1024]{3,2,1,0:T(2,128)S(1)} copy-done((f32[16,2,2,1024]{3,2,1,0:T(2,128)S(1)}, f32[16,2,2,1024]{3,2,1,0:T(2,128)}, u32[]{:S(2)}) %copy-start.1) | copy-done | bytes 262168
  1.6 0.0 copy-start.2
  1.6 0.9 %copy-done.2 = f32[16,2,2,1024]{3,2,1,0:T(2,128)S(1)} copy-done((f32[16,2,2,1024]{3,2,1,0:T(2,128)S(1)}, f32[16,2,2,1024]{3,2,1,0:T(2,128)}, u32[]{:S(2)}) %copy-start.2) | copy-done | bytes 262168
  2.5 0.0 copy-start.3
  2.5 0.9 %copy-done.3 = f32[16,2,2,1024]{3,2,1,0:T(2,128)S(1)} copy-done((f32[16,2,2,1024]{3,2,1,0:T(2,128)S(1)}, f32[16,2,2,1024]{3,2,1,0:T(2,128)}, u32[]{:S(2)}) %copy-start.3) | copy-done | bytes 262168
  3.5 0.0 copy-start.4
  3.5 0.9 %copy-done.4 = f32[16,2,1024]{2,1,0:T(2,128)S(1)} copy-done((f32[16,2,1024]{2,1,0:T(2,128)S(1)}, f32[16,2,1024]{2,1,0:T(2,128)}, u32[]{:S(2)}) %copy-start.4) | copy-done | bytes 131096
  4.4 0.0 copy-start.6
  4.4 0.8 %copy-done.6 = f32[16,1024]{1,0:T(8,128)S(1)} copy-done((f32[16,1024]{1,0:T(8,128)S(1)}, f32[16,1024]{1,0:T(8,128)}, u32[]{:S(2)}) %copy-start.6) | copy-done | bytes 65560
  5.2 0.8 %copy-done.7 = s32[16,1024]{1,0:T(8,128)S(1)} copy-done((s32[16,1024]{1,0:T(8,128)S(1)}, s32[16,1024]{1,0:T(8,128)}, u32[]{:S(2)}) %copy-start.7) | copy-done | bytes 65560
  6.1 0.8 %copy-done.8 = s32[1,1,16,1024,1]{3,4,2,1,0:T(1,128)S(1)} copy-done((s32[1,1,16,1024,1]{3,4,2,1,0:T(1,128)S(1)}, s32[1,1,16,1024,1]{3,4,2,1,0:T(1,128)}, u32[]{:S(2)}) %copy-start.8) | copy-done | bytes 65560
  6.9 0.8 %copy-done.9 = s32[16,1024]{1,0:T(8,128)S(1)} copy-done((s32[16,1024]{1,0:T(8,128)S(1)}, s32[16,1024]{1,0:T(8,128)}, u32[]{:S(2)}) %copy-start.9) | copy-done | bytes 65560
  7.8 0.8 %copy-done.10 = s32[16,1024]{1,0:T(8,128)S(1)} copy-done((s32[16,1024]{1,0:T(8,128)S(1)}, s32[16,1024]{1,0:T(8,128)}, u32[]{:S(2)}) %copy-start.10) | copy-done | bytes 65560
  8.6 0.8 %copy-done.11 = f32[32,512]{1,0:T(8,128)S(1)} copy-done((f32[32,512]{1,0:T(8,128)S(1)}, f32[32,512]{1,0:T(8,128)}, u32[]{:S(2)}) %copy-start.11) | copy-done | bytes 65560
  9.4 0.8 %copy-done.12 = f32[32,512]{1,0:T(8,128)S(1)} copy-done((f32[32,512]{1,0:T(8,128)S(1)}, f32[32,512]{1,0:T(8,128)}, u32[]{:S(2)}) %copy-start.12) | copy-done | bytes 65560
  10.3 0.8 %copy-done.13 = f32[32,512]{1,0:T(8,128)S(1)} copy-done((f32[32,512]{1,0:T(8,128)S(1)}, f32[32,512]{1,0:T(8,128)}, u32[]{:S(2)}) %copy-start.13) | copy-done | bytes 65560
  11.1 0.8 %copy-done.14 = f32[32,512]{1,0:T(8,128)S(1)} copy-done((f32[32,512]{1,0:T(8,128)S(1)}, f32[32,512]{1,0:T(8,128)}, u32[]{:S(2)}) %copy-start.14) | copy-done | bytes 65560
  12.0 0.8 %copy-done.15 = s32[32,512]{1,0:T(8,128)S(1)} copy-done((s32[32,512]{1,0:T(8,128)S(1)}, s32[32,512]{1,0:T(8,128)}, u32[]{:S(2)}) %copy-start.15) | copy-done | bytes 65560
  12.8 50.1 %step.1 = (f32[16,16,128]{2,1,0:T(8,128)S(1)}, f32[5,48,768]{2,1,0:T(8,128)S(1)}) custom-call(f32[16,2,16,128]{3,2,1,0:T(8,128)S(1)} %bitcast.26, f32[16,2,16,128]{3,2,1,0:T(8,128)S(1)} %bitcast.27, f32[16,2,16,128]{3,2,1,0:T(8,128)S(1)} %bitcast.28, f32[16,16,128]{2,1,0:T(8,128)S(1)} %bitcast.29, f32[16,1024]{1,0:T(8,128)S(1)} %copy-done.6, ...), custom_call_target="tpu_custom_call" | custom-call | tf_op jit(solution)/shard_map/step/pallas_call | solution.py:441
  62.9 0.0 copy-start
  62.9 0.9 %copy-done = f32[5,48,768]{2,1,0:T(8,128)} copy-done((f32[5,48,768]{2,1,0:T(8,128)}, f32[5,48,768]{2,1,0:T(8,128)S(1)}, u32[]{:S(2)}) %copy-start) | copy-done | bytes 737304
  63.8 0.6 copy-done.5
  64.5 6.9 %flood.1 = (f32[32,512]{1,0:T(8,128)}, f32[32,512]{1,0:T(8,128)}, f32[32,512]{1,0:T(8,128)}, f32[16,16,128]{2,1,0:T(8,128)}) custom-call(f32[5,48,768]{2,1,0:T(8,128)} %copy-done, f32[16,16,128]{2,1,0:T(8,128)} %copy-done.5), custom_call_target="tpu_custom_call" | custom-call | tf_op jit(solution)/shard_map/flood/pallas_call | solution.py:515
  (10 shorter events, 0.0 us)
Async XLA Ops:
  0.6 1.0 %copy-start.1 = (f32[16,2,2,1024]{3,2,1,0:T(2,128)S(1)}, f32[16,2,2,1024]{3,2,1,0:T(2,128)}, u32[]{:S(2)}) copy-start(f32[16,2,2,1024]{3,2,1,0:T(2,128)} %param.14) | copy-start | bytes 786436
  1.6 0.9 %copy-start.2 = (f32[16,2,2,1024]{3,2,1,0:T(2,128)S(1)}, f32[16,2,2,1024]{3,2,1,0:T(2,128)}, u32[]{:S(2)}) copy-start(f32[16,2,2,1024]{3,2,1,0:T(2,128)} %param.15) | copy-start | bytes 786436
  2.5 0.9 %copy-start.3 = (f32[16,2,2,1024]{3,2,1,0:T(2,128)S(1)}, f32[16,2,2,1024]{3,2,1,0:T(2,128)}, u32[]{:S(2)}) copy-start(f32[16,2,2,1024]{3,2,1,0:T(2,128)} %param.16) | copy-start | bytes 786436
  3.5 0.9 %copy-start.4 = (f32[16,2,1024]{2,1,0:T(2,128)S(1)}, f32[16,2,1024]{2,1,0:T(2,128)}, u32[]{:S(2)}) copy-start(f32[16,2,1024]{2,1,0:T(2,128)} %param.17) | copy-start | bytes 393220
  4.4 0.8 %copy-start.6 = (f32[16,1024]{1,0:T(8,128)S(1)}, f32[16,1024]{1,0:T(8,128)}, u32[]{:S(2)}) copy-start(f32[16,1024]{1,0:T(8,128)} %crest_ref.1) | copy-start | bytes 196612
  5.2 0.8 %copy-start.7 = (s32[16,1024]{1,0:T(8,128)S(1)}, s32[16,1024]{1,0:T(8,128)}, u32[]{:S(2)}) copy-start(s32[16,1024]{1,0:T(8,128)} %regime_ref.1) | copy-start | bytes 196612
  6.1 0.8 %copy-start.8 = (s32[1,1,16,1024,1]{3,4,2,1,0:T(1,128)S(1)}, s32[1,1,16,1024,1]{3,4,2,1,0:T(1,128)}, u32[]{:S(2)}) copy-start(s32[1,1,16,1024,1]{3,4,2,1,0:T(1,128)} %param.20) | copy-start | bytes 196612
  6.9 0.8 %copy-start.9 = (s32[16,1024]{1,0:T(8,128)S(1)}, s32[16,1024]{1,0:T(8,128)}, u32[]{:S(2)}) copy-start(s32[16,1024]{1,0:T(8,128)} %row_ref.1) | copy-start | bytes 196612
  7.8 0.8 %copy-start.10 = (s32[16,1024]{1,0:T(8,128)S(1)}, s32[16,1024]{1,0:T(8,128)}, u32[]{:S(2)}) copy-start(s32[16,1024]{1,0:T(8,128)} %col_ref.1) | copy-start | bytes 196612
  8.6 0.8 %copy-start.11 = (f32[32,512]{1,0:T(8,128)S(1)}, f32[32,512]{1,0:T(8,128)}, u32[]{:S(2)}) copy-start(f32[32,512]{1,0:T(8,128)} %bed_ref.1) | copy-start | bytes 196612
  9.4 0.8 %copy-start.12 = (f32[32,512]{1,0:T(8,128)S(1)}, f32[32,512]{1,0:T(8,128)}, u32[]{:S(2)}) copy-start(f32[32,512]{1,0:T(8,128)} %depth_ref.1) | copy-start | bytes 196612
  10.3 0.8 %copy-start.13 = (f32[32,512]{1,0:T(8,128)S(1)}, f32[32,512]{1,0:T(8,128)}, u32[]{:S(2)}) copy-start(f32[32,512]{1,0:T(8,128)} %one_ref.1) | copy-start | bytes 196612
  11.1 0.8 %copy-start.14 = (f32[32,512]{1,0:T(8,128)S(1)}, f32[32,512]{1,0:T(8,128)}, u32[]{:S(2)}) copy-start(f32[32,512]{1,0:T(8,128)} %two_ref.1) | copy-start | bytes 196612
  12.0 0.8 %copy-start.15 = (s32[32,512]{1,0:T(8,128)S(1)}, s32[32,512]{1,0:T(8,128)}, u32[]{:S(2)}) copy-start(s32[32,512]{1,0:T(8,128)} %mask_ref.1) | copy-start | bytes 196612
  62.9 0.9 %copy-start = (f32[5,48,768]{2,1,0:T(8,128)}, f32[5,48,768]{2,1,0:T(8,128)S(1)}, u32[]{:S(2)}) copy-start(f32[5,48,768]{2,1,0:T(8,128)S(1)} %get-tuple-element.10.field) | copy-start | bytes 2211844
  63.8 0.6 copy-start.5

commit v2 on v1

--- a/solution.py
+++ b/solution.py
@@ -21,6 +21,7 @@
 SUB = 8
 MESH = pl.DeviceIdType.MESH
 VMEM_SPEC = pl.BlockSpec(memory_space=pltpu.VMEM)
+HBM_SPEC = pl.BlockSpec(memory_space=pltpu.HBM)
 f32 = jnp.float32
 bf16 = jnp.bfloat16
 i32 = jnp.int32
@@ -145,15 +146,25 @@
 
 
 def step_kernel(
-    n_row, n_col,
-    lower_ref, main_ref, upper_ref, rhs_ref, crest_ref, regime_ref, tile_ref, row_ref, col_ref,
-    bed_ref, depth_ref, one_ref, two_ref, mask_ref,
-    state_ref, field,
+    n_row, n_col, *refs
+):
+    inputs, (state_ref, field), fetched = refs[:14], refs[14:16], refs[16:30]
+    (
     couple, local, heads, head_in, edges, edge_in, crest, regime, cells, tiles, earlier,
-    hot, ranks, left, total, pieces, slots, land, one_hot, two_hot, scatter,
+    hot, ranks, left, left_two, total, pieces, slots, land, one_hot, two_hot, scatter,
     ready, send_one, recv_one, send_two, recv_two, send_all, recv_all,
-    send_fix, recv_fix, send_wet, recv_wet,
-):
+    send_fix, recv_fix, send_wet, recv_wet, fetch,
+    ) = refs[30:]
+    (
+        lower_ref, main_ref, upper_ref, rhs_ref, crest_ref, regime_ref, tile_ref, row_ref, col_ref,
+        bed_ref, depth_ref, one_ref, two_ref, mask_ref,
+    ) = fetched
+    loads = [
+        pltpu.make_async_copy(source, target, fetch.at[k])
+        for k, (source, target) in enumerate(zip(inputs, fetched))
+    ]
+    for load in loads:
+        load.start()
     sections = rhs_ref.shape[0]
     height, width = bed_ref.shape
     devices = n_row * n_col
@@ -169,6 +180,8 @@
     for device in col_peers:
         pl.semaphore_signal(barrier, inc=1, device_id=device, device_id_type=MESH)
 
+    for load in loads[:4]:
+        load.wait()
     solve_local(sections, lower_ref, main_ref, upper_ref, rhs_ref, couple, local, heads)
 
     pl.semaphore_wait(barrier, n_row + n_col - 2)
@@ -190,6 +203,8 @@
     for device in col_peers:
         pl.semaphore_signal(ready, inc=1, device_id=device, device_id_type=MESH)
 
+    for load in loads[4:]:
+        load.wait()
     for half in range(sections // SUB):
         for k in range(SUB):
             rows, cols = pl.ds(half * SUB, SUB), pl.ds(k * LANES, LANES)
@@ -198,7 +213,9 @@
             col = col_ref[rows, cols]
             cells[0, rows, k, :] = (row_ref[rows, cols] + (col >> 8) * height).astype(f32)
             cells[1, rows, k, :] = (col & 255).astype(f32)
-    tiles[...] = (tile_ref[...] - me + devices) & (devices - 1)
+    step_row = (lax.div(tile_ref[...], n_col) - my_row) & (n_row - 1)
+    step_col = (lax.rem(tile_ref[...], n_col) - my_col) & (n_col - 1)
+    tiles[...] = step_row + n_row * step_col
     wide = 2 * LANES
     earlier[...] = (
         lax.broadcasted_iota(i32, (wide, wide), 0) < lax.broadcasted_iota(i32, (wide, wide), 1)
@@ -207,7 +224,7 @@
     tile_table = lax.broadcasted_iota(i32, (devices, wide), 0)
     rank_table = lax.broadcasted_iota(i32, (capacity, wide), 0).astype(f32)
 
-    def rank_step(index, offset):
+    def rank_build(index, offset, side):
         here = tiles[pl.ds(pl.multiple_of(index * SUB, SUB), SUB), :]
         for part in range(CHUNK // wide):
             lanes = pl.ds(part * wide, wide)
@@ -220,9 +237,28 @@
             rank = jnp.sum(jnp.where(mine, base, 0.0), axis=0, keepdims=True)
             offset = offset + counts
             ranks[index, :, lanes] = jnp.where(rank == rank_table, 1.0, 0.0).astype(bf16)
+            for q in range(2):
+                row = jnp.broadcast_to(both(cells[q, index], 2 * part), (devices, wide)).astype(bf16)
+                side[pl.ds(q * devices, devices), lanes] = mine_one * row
         return offset
 
-    lax.fori_loop(0, chunks, rank_step, jnp.zeros((devices, LANES), f32))
+    def multiply(side, index, extent):
+        used = pl.ds(0, extent * devices)
+        total[used] += nt_dot(side[used], ranks[index])
+
+    def rank_step(index, offset):
+        at = index * 2
+        offset = rank_build(at, offset, left)
+        multiply(left_two, lax.rem(at + chunks - 1, chunks), 2)
+        offset = rank_build(at + 1, offset, left_two)
+        multiply(left, at, 2)
+        return offset
+
+    total[: 2 * devices] = jnp.zeros((2 * devices, capacity), f32)
+    left_two[: 2 * devices] = jnp.zeros((2 * devices, CHUNK), bf16)
+    ranks[chunks - 1] = jnp.zeros((capacity, CHUNK), bf16)
+    first_part = chunks * 3 // 16
+    offset = lax.fori_loop(0, first_part, rank_step, jnp.zeros((devices, LANES), f32))
     for copy in copies:
         copy.wait()
 
@@ -233,31 +269,6 @@
     for q, ref in enumerate((bed_ref, one_ref, two_ref)):
         field[(1 + q,) + inner] = ref[...]
     field[(4,) + inner] = mask_ref[...].astype(f32)
-
-    def fill(index, values, offsets, extent):
-        for part in range(CHUNK // wide):
-            lanes = pl.ds(part * wide, wide)
-            mine = hot[index, offsets, lanes]
-            for q, value in enumerate(values):
-                row = jnp.broadcast_to(both(value, 2 * part), (extent, wide)).astype(bf16)
-                left[pl.ds(q * extent, extent), lanes] = mine * row
-        total[...] += nt_dot(left[...], ranks[index])
-
-    def put(slot, offsets, value):
-        slots[offsets, slot, :] = value[:, :LANES]
-        slots[offsets, slot + 1, :] = value[:, LANES:]
-
-    total[...] = jnp.zeros_like(total)
-
-    def cell_step(index, carry):
-        fill(index, [cells[0, index], cells[1, index]], pl.ds(0, devices), devices)
-        return carry
-
-    lax.fori_loop(0, chunks, cell_step, 0)
-    put(4, pl.ds(0, devices), total[pl.ds(0, devices), :] * 256.0 + total[pl.ds(devices, devices), :])
-    pl.semaphore_wait(ready, n_col - 1)
-    for copy in copies:
-        copy.wait()
 
     around = [(a, b) for a in (-1, 0, 1) for b in (-1, 0, 1) if (a, b) != (0, 0)]
 
@@ -282,7 +293,41 @@
             sent.append(copy)
         return sent
 
+    pl.semaphore_wait(ready, n_col - 1)
     fixed = halo(pl.ds(1, 4), send_fix, recv_fix)
+    lax.fori_loop(first_part, chunks // 2, rank_step, offset)
+    multiply(left_two, chunks - 1, 2)
+
+    def build(left, index, source, extent):
+        for part in range(CHUNK // wide):
+            lanes = pl.ds(part * wide, wide)
+            mine = hot[index, :, lanes]
+            for q in range(extent):
+                row = jnp.broadcast_to(both(source[q, index], 2 * part), (devices, wide)).astype(bf16)
+                left[pl.ds(q * devices, devices), lanes] = mine * row
+
+    def fill(source, extent):
+        total[: extent * devices] = jnp.zeros((extent * devices, capacity), f32)
+        build(left, 0, source, extent)
+
+        def fill_step(index, carry):
+            at = index * 2
+            build(left_two, at + 1, source, extent)
+            multiply(left, at, extent)
+            build(left, lax.rem(at + 2, chunks), source, extent)
+            multiply(left_two, at + 1, extent)
+            return carry
+
+        lax.fori_loop(0, chunks // 2, fill_step, 0)
+
+    def put(slot, offsets, value):
+        slots[offsets, slot, :] = value[:, :LANES]
+        slots[offsets, slot + 1, :] = value[:, LANES:]
+
+    put(4, pl.ds(0, devices), total[pl.ds(0, devices), :] * 256.0 + total[pl.ds(devices, devices), :])
+    for copy in copies:
+        copy.wait()
+
 
     before = [edge_in[:, q, :] for q in range(2)]
     behind = [edge_in[:, 2 + q, :] for q in range(2)]
@@ -307,35 +352,24 @@
             pieces[q, s] = piece
 
     def send_slot(k):
-        peer = lax.rem(me + k, devices)
+        a, b = lax.rem(k, n_row), k // n_row
+        to_row, to_col = lax.rem(my_row + a, n_row), lax.rem(my_col + b, n_col)
         return pltpu.make_async_remote_copy(
             src_ref=slots.at[k], dst_ref=land.at[k],
             send_sem=send_all.at[k // SUB], recv_sem=recv_all.at[k // SUB],
-            device_id=(peer // n_col, lax.rem(peer, n_col)), device_id_type=MESH,
+            device_id=(to_row, to_col), device_id_type=MESH,
         )
 
-    per_step = HALF // chunks
-    for side in range(devices // HALF):
-        offsets = pl.ds(side * HALF, HALF)
-        total[...] = jnp.zeros_like(total)
-
-        def value_step(index, carry):
-            if side > 0:
-                for j in range(per_step):
-                    k = (side - 1) * HALF + index * per_step + j
-                    if j == 0 and side == 1:
-                        @pl.when(index > 0)
-                        def _():
-                            send_slot(k).start()
-                    else:
-                        send_slot(k).start()
-            fill(index, [pieces[q, index] for q in range(4)], offsets, HALF)
-            return carry
-
-        lax.fori_loop(0, chunks, value_step, 0)
-        piece = lambda q: total[pl.ds(q * HALF, HALF), :]
-        put(0, offsets, piece(0) + piece(1))
-        put(2, offsets, piece(2) + piece(3))
+    fill(pieces, 4)
+    piece = lambda q: total[pl.ds(q * devices, devices), :]
+    put(0, pl.ds(0, devices), piece(0) + piece(1))
+    put(2, pl.ds(0, devices), piece(2) + piece(3))
+
+    def send_step(k, carry):
+        send_slot(k).start()
+        return carry
+
+    lax.fori_loop(1, devices, send_step, 0)
     land[0] = slots[0]
 
     cells_one, cells_two = 2 * height, 256
@@ -370,9 +404,7 @@
         scatter[...] += nt_dot(one_hot[...], two_hot[...])
 
     groups = devices // SUB
-    def early_step(index, carry):
-        for j in range(SUB):
-            send_slot(devices - HALF + index * SUB + j).start()
+    def late_step(index, carry):
         @pl.when(index == 0)
         def _():
             arrive(1, SUB - 1, 0)
@@ -382,14 +414,7 @@
         apply_step(index)
         return carry
 
-    lax.fori_loop(0, HALF // SUB, early_step, 0)
-
-    def late_step(index, carry):
-        arrive(index * SUB, SUB, index)
-        apply_step(index)
-        return carry
-
-    lax.fori_loop(HALF // SUB, groups, late_step, 0)
+    lax.fori_loop(0, groups, late_step, 0)
 
     piece = lambda q, side: scatter[pl.ds(q * cells_one + side * height, height), :]
     for side in range(2):
@@ -434,6 +459,10 @@
     devices = n_row * n_col
     capacity = 2 * row.size // devices
     chunks = row.size // CHUNK
+    operands = (
+        dense(lower), dense(main), dense(upper), dense(rhs), crest, regime,
+        tile.reshape(-1, LANES), row, col, bed, depth, one, two, mask,
+    )
     wide = lambda *lead: pltpu.VMEM(lead + (SUB, LANES), f32)
     vmem = lambda *shape: pltpu.VMEM(shape, f32)
     half = lambda *shape: pltpu.VMEM(shape, bf16)
@@ -444,29 +473,27 @@
             jax.ShapeDtypeStruct((sections, 2 * SUB, LANES), f32),
             jax.ShapeDtypeStruct((5, height + 2 * SUB, width + 2 * LANES), f32),
         ),
-        in_specs=[VMEM_SPEC] * 14,
+        in_specs=[HBM_SPEC] * 14,
         out_specs=(VMEM_SPEC,) * 2,
-        scratch_shapes=[
+        scratch_shapes=[pltpu.VMEM(x.shape, x.dtype) for x in operands]
+        + [
             wide(sections, 4), wide(sections, 10),
             vmem(n_row, 24, LANES), vmem(n_row, 24, LANES), wide(n_row), wide(n_row),
             wide(sections), pltpu.VMEM((sections, SUB, LANES), i32), wide(2, sections),
             pltpu.VMEM((row.size // LANES, LANES), i32), half(2 * LANES, 2 * LANES),
             half(chunks, devices, CHUNK), half(chunks, capacity, CHUNK),
-            half(4 * HALF, CHUNK), vmem(4 * HALF, capacity), wide(4, sections),
+            half(4 * devices, CHUNK), half(4 * devices, CHUNK), vmem(4 * devices, capacity), wide(4, sections),
             vmem(devices, 6, LANES), vmem(devices, 6, LANES),
             half(8 * height, SUB * capacity), half(256, SUB * capacity), vmem(8 * height, 256),
             pltpu.SemaphoreType.REGULAR,
             dma(n_row - 1), dma(n_row - 1), dma(n_row - 1), dma(n_row - 1),
-            dma(devices // SUB), dma(devices // SUB), dma(8), dma(8), dma(8), dma(8),
+            dma(devices // SUB), dma(devices // SUB), dma(8), dma(8), dma(8), dma(8), dma(14),
         ],
         compiler_params=pltpu.CompilerParams(
-            collective_id=0, has_side_effects=True, vmem_limit_bytes=40 << 20
+            collective_id=0, has_side_effects=True, vmem_limit_bytes=60 << 20
         ),
         name="step",
-    )(
-        dense(lower), dense(main), dense(upper), dense(rhs), crest, regime,
-        tile.reshape(-1, LANES), row, col, bed, depth, one, two, mask,
-    )
+    )(*operands)
 
 
 def face_flux(surface, after, bed, bed_after, old):
@@ -476,9 +503,8 @@
     return pushed / (1.0 + (GRAVITY * TIME_STEP * MANNING_SQ) * jnp.abs(old) * drag)
 
 
-def flood_kernel(n_row, n_col, field, state_ref, depth_out, one_out, two_out, state_out, sem):
-    copy = pltpu.make_async_copy(state_ref, state_out, sem)
-    copy.start()
+def flood_kernel(n_row, n_col, field, state_ref, depth_out, one_out, two_out, state_out):
+    state_out[...] = state_ref[...]
     height, width = depth_out.shape
     my_row, my_col = lax.axis_index("row"), lax.axis_index("col")
     depth, bed, one, two, mask = [field[q] for q in range(5)]
@@ -508,7 +534,6 @@
     depth_out[...] = depth[inner]
     one_out[...] = one[inner]
     two_out[...] = two[inner]
-    copy.wait()
 
 
 def flood(field, state, shape, n_row, n_col):
@@ -516,9 +541,8 @@
         functools.partial(flood_kernel, n_row, n_col),
         out_shape=(jax.ShapeDtypeStruct(shape, f32),) * 3
         + (jax.ShapeDtypeStruct(state.shape, f32),),
-        in_specs=[VMEM_SPEC, pl.BlockSpec(memory_space=pl.ANY)],
-        out_specs=(VMEM_SPEC,) * 3 + (pl.BlockSpec(memory_space=pl.ANY),),
-        scratch_shapes=[pltpu.SemaphoreType.DMA],
+        in_specs=[VMEM_SPEC] * 2,
+        out_specs=(VMEM_SPEC,) * 4,
         name="flood",
     )(field, state)
 

time: 72.1 us -> 47.7 us (0.66)
  local copies, waits for them, and re-layouts: 13.7 us -> 0 us
  Pallas kernels: 57 us -> 46.9 us
    unnamed x32 -> x0, local copies, waits for them, and re-layouts: 13.7 us -> none
    pallas_call x1, Pallas kernels: 50.1 us -> 44.6 us  [whole_step(): pl.pallas_call(functools.partial(step_kernel, n_row, n_col), out_shape=(j...]
    pallas_call x1, Pallas kernels: 6.87 us -> 2.3 us  [flood(): pl.pallas_call(functools.partial(flood_kernel, n_row, n_col), out_shape=(...]
where the time goes in v2:
time: 47.7 us; the launch traced here: 47.6 us
  Pallas kernels  46.9 us (98%)
  between operations  0.64 us (1%)
    pallas_call x1, Pallas kernels, whole_step(): pl.pallas_call(functools.partial(step_kernel, n_row, n_col), out_shape=(j...  44.6 us
    pallas_call x1, Pallas kernels, flood(): pl.pallas_call(functools.partial(flood_kernel, n_row, n_col), out_shape=(...  2.3 us

profile of v2, /device:TPU:1, one launch (start us, length us, event | category | flops | bytes accessed | tf_op | source)
XLA Modules:
  0.0 47.6 jit_solution(10621805369180201708)
XLA Ops:
  0.6 44.6 %step.1 = (f32[16,16,128]{2,1,0:T(8,128)}, f32[5,48,768]{2,1,0:T(8,128)}) custom-call(f32[16,2,16,128]{3,2,1,0:T(8,128)} %bitcast.26, f32[16,2,16,128]{3,2,1,0:T(8,128)} %bitcast.27, f32[16,2,16,128]{3,2,1,0:T(8,128)} %bitcast.28, f32[16,16,128]{2,1,0:T(8,128)} %bitcast.29, f32[16,1024]{1,0:T(8,128)} %refs_4_.1, s32[16,1024]{1,0:T(8,128)} %refs_5_.1, ...), custom_call_target="tpu_custom_call" | custom-call | tf_op jit(solution)/shard_map/step/pallas_call | solution.py:470
  45.3 2.3 %flood.1 = (f32[32,512]{1,0:T(8,128)}, f32[32,512]{1,0:T(8,128)}, f32[32,512]{1,0:T(8,128)}, f32[16,16,128]{2,1,0:T(8,128)}) custom-call(f32[5,48,768]{2,1,0:T(8,128)} %get-tuple-element.10.field, f32[16,16,128]{2,1,0:T(8,128)} %get-tuple-element.11.state_ref), custom_call_target="tpu_custom_call" | custom-call | tf_op jit(solution)/shard_map/flood/pallas_call | solution.py:540

commit v3 on v2

--- a/solution.py
+++ b/solution.py
@@ -218,28 +218,28 @@
     tiles[...] = step_row + n_row * step_col
     wide = 2 * LANES
     earlier[...] = (
-        lax.broadcasted_iota(i32, (wide, wide), 0) < lax.broadcasted_iota(i32, (wide, wide), 1)
+        lax.broadcasted_iota(i32, (wide, wide), 0) <= lax.broadcasted_iota(i32, (wide, wide), 1)
     ).astype(f32).astype(bf16)
-    every = jnp.ones((wide, LANES), bf16)
     tile_table = lax.broadcasted_iota(i32, (devices, wide), 0)
-    rank_table = lax.broadcasted_iota(i32, (capacity, wide), 0).astype(f32)
+    rank_table = (lax.broadcasted_iota(i32, (capacity, wide), 0) + 1).astype(f32).astype(bf16)
 
     def rank_build(index, offset, side):
         here = tiles[pl.ds(pl.multiple_of(index * SUB, SUB), SUB), :]
-        for part in range(CHUNK // wide):
+        parts = range(CHUNK // wide)
+        mine = [both(here, 2 * part) == tile_table for part in parts]
+        ones = [jnp.where(m, 1.0, 0.0).astype(bf16) for m in mine]
+        upto = jnp.dot(jnp.concatenate(ones, axis=0), earlier[...], preferred_element_type=f32)
+        for part in parts:
             lanes = pl.ds(part * wide, wide)
-            mine = both(here, 2 * part) == tile_table
-            mine_one = jnp.where(mine, 1.0, 0.0).astype(bf16)
-            hot[index, :, lanes] = mine_one
-            within = jnp.dot(mine_one, earlier[...], preferred_element_type=f32)
-            counts = jnp.dot(mine_one, every, preferred_element_type=f32)
-            base = within + jnp.concatenate([offset, offset], axis=1)
-            rank = jnp.sum(jnp.where(mine, base, 0.0), axis=0, keepdims=True)
-            offset = offset + counts
-            ranks[index, :, lanes] = jnp.where(rank == rank_table, 1.0, 0.0).astype(bf16)
+            hot[index, :, lanes] = ones[part]
+            count = upto[part * devices : (part + 1) * devices]
+            base = count + jnp.concatenate([offset, offset], axis=1)
+            rank = jnp.sum(jnp.where(mine[part], base, 0.0), axis=0, keepdims=True)
+            offset = offset + jnp.broadcast_to(count[:, wide - 1 :], (devices, LANES))
+            ranks[index, :, lanes] = jnp.where(rank.astype(bf16) == rank_table, bf16(1.0), bf16(0.0))
             for q in range(2):
                 row = jnp.broadcast_to(both(cells[q, index], 2 * part), (devices, wide)).astype(bf16)
-                side[pl.ds(q * devices, devices), lanes] = mine_one * row
+                side[pl.ds(q * devices, devices), lanes] = ones[part] * row
         return offset
 
     def multiply(side, index, extent):
@@ -405,16 +405,13 @@
 
     groups = devices // SUB
     def late_step(index, carry):
-        @pl.when(index == 0)
-        def _():
-            arrive(1, SUB - 1, 0)
-        @pl.when(index > 0)
-        def _():
-            arrive(index * SUB, SUB, index)
+        arrive(index * SUB, SUB, index)
         apply_step(index)
         return carry
 
-    lax.fori_loop(0, groups, late_step, 0)
+    arrive(1, SUB - 1, 0)
+    apply_step(0)
+    lax.fori_loop(1, groups, late_step, 0)
 
     piece = lambda q, side: scatter[pl.ds(q * cells_one + side * height, height), :]
     for side in range(2):

time: 47.7 us -> 46.7 us (0.979)
  Pallas kernels: 46.9 us -> 45.9 us
    pallas_call x1, Pallas kernels: 44.6 us -> 43.6 us  [whole_step(): pl.pallas_call(functools.partial(step_kernel, n_row, n_col), out_shape=(j...]
where the time goes in v3:
time: 46.7 us; the launch traced here: 46.6 us
  Pallas kernels  45.9 us (98%)
  between operations  0.64 us (1%)
    pallas_call x1, Pallas kernels, whole_step(): pl.pallas_call(functools.partial(step_kernel, n_row, n_col), out_shape=(j...  43.6 us
    pallas_call x1, Pallas kernels, flood(): pl.pallas_call(functools.partial(flood_kernel, n_row, n_col), out_shape=(...  2.3 us

profile of v3, /device:TPU:1, one launch (start us, length us, event | category | flops | bytes accessed | tf_op | source)
XLA Modules:
  0.0 46.6 jit_solution(16251307109344287819)
XLA Ops:
  0.6 43.6 %step.1 = (f32[16,16,128]{2,1,0:T(8,128)}, f32[5,48,768]{2,1,0:T(8,128)}) custom-call(f32[16,2,16,128]{3,2,1,0:T(8,128)} %bitcast.26, f32[16,2,16,128]{3,2,1,0:T(8,128)} %bitcast.27, f32[16,2,16,128]{3,2,1,0:T(8,128)} %bitcast.28, f32[16,16,128]{2,1,0:T(8,128)} %bitcast.29, f32[16,1024]{1,0:T(8,128)} %refs_4_.1, s32[16,1024]{1,0:T(8,128)} %refs_5_.1, ...), custom_call_target="tpu_custom_call" | custom-call | tf_op jit(solution)/shard_map/step/pallas_call | solution.py:467
  44.3 2.3 %flood.1 = (f32[32,512]{1,0:T(8,128)}, f32[32,512]{1,0:T(8,128)}, f32[32,512]{1,0:T(8,128)}, f32[16,16,128]{2,1,0:T(8,128)}) custom-call(f32[5,48,768]{2,1,0:T(8,128)} %get-tuple-element.10.field, f32[16,16,128]{2,1,0:T(8,128)} %get-tuple-element.11.state_ref), custom_call_target="tpu_custom_call" | custom-call | tf_op jit(solution)/shard_map/flood/pallas_call | solution.py:537

commit v4 on v3

--- a/solution.py
+++ b/solution.py
@@ -57,8 +57,9 @@
     return [m[3] * scale, -(m[1] * scale), -(m[2] * scale), m[0] * scale]
 
 
-CHUNK = 1024
-HALF = 64
+CHUNK = 2048
+ROWS = CHUNK // LANES
+GROUP = 16
 
 
 def split_two(x):
@@ -68,6 +69,11 @@
 
 def both(x, row):
     return jnp.concatenate([x[row : row + 1, :], x[row + 1 : row + 2, :]], axis=1)
+
+
+def pair_at(ref, q, index, part):
+    each = SUB // 2
+    return both(ref[q, index * (ROWS // SUB) + part // each], 2 * (part % each))
 
 
 def nt_dot(left, right):
@@ -224,7 +230,7 @@
     rank_table = (lax.broadcasted_iota(i32, (capacity, wide), 0) + 1).astype(f32).astype(bf16)
 
     def rank_build(index, offset, side):
-        here = tiles[pl.ds(pl.multiple_of(index * SUB, SUB), SUB), :]
+        here = tiles[pl.ds(pl.multiple_of(index * ROWS, ROWS), ROWS), :]
         parts = range(CHUNK // wide)
         mine = [both(here, 2 * part) == tile_table for part in parts]
         ones = [jnp.where(m, 1.0, 0.0).astype(bf16) for m in mine]
@@ -238,7 +244,7 @@
             offset = offset + jnp.broadcast_to(count[:, wide - 1 :], (devices, LANES))
             ranks[index, :, lanes] = jnp.where(rank.astype(bf16) == rank_table, bf16(1.0), bf16(0.0))
             for q in range(2):
-                row = jnp.broadcast_to(both(cells[q, index], 2 * part), (devices, wide)).astype(bf16)
+                row = jnp.broadcast_to(pair_at(cells, q, index, part), (devices, wide)).astype(bf16)
                 side[pl.ds(q * devices, devices), lanes] = ones[part] * row
         return offset
 
@@ -257,7 +263,7 @@
     total[: 2 * devices] = jnp.zeros((2 * devices, capacity), f32)
     left_two[: 2 * devices] = jnp.zeros((2 * devices, CHUNK), bf16)
     ranks[chunks - 1] = jnp.zeros((capacity, CHUNK), bf16)
-    first_part = chunks * 3 // 16
+    first_part = chunks // 4
     offset = lax.fori_loop(0, first_part, rank_step, jnp.zeros((devices, LANES), f32))
     for copy in copies:
         copy.wait()
@@ -303,7 +309,7 @@
             lanes = pl.ds(part * wide, wide)
             mine = hot[index, :, lanes]
             for q in range(extent):
-                row = jnp.broadcast_to(both(source[q, index], 2 * part), (devices, wide)).astype(bf16)
+                row = jnp.broadcast_to(pair_at(source, q, index, part), (devices, wide)).astype(bf16)
                 left[pl.ds(q * devices, devices), lanes] = mine * row
 
     def fill(source, extent):
@@ -356,7 +362,7 @@
         to_row, to_col = lax.rem(my_row + a, n_row), lax.rem(my_col + b, n_col)
         return pltpu.make_async_remote_copy(
             src_ref=slots.at[k], dst_ref=land.at[k],
-            send_sem=send_all.at[k // SUB], recv_sem=recv_all.at[k // SUB],
+            send_sem=send_all.at[k // GROUP], recv_sem=recv_all.at[k // GROUP],
             device_id=(to_row, to_col), device_id_type=MESH,
         )
 
@@ -385,15 +391,15 @@
         ).wait_recv()
 
     def apply_step(index):
-        first_slot = pl.multiple_of(index * SUB, SUB)
-        here = [land[pl.ds(first_slot, SUB), q, :] for q in range(6)]
+        first_slot = pl.multiple_of(index * GROUP, GROUP)
+        here = [land[pl.ds(first_slot, GROUP), q, :] for q in range(6)]
         cell = here[4:]
         first = [jnp.floor(c * (1.0 / 256.0)) for c in cell]
         second = [c - f * 256.0 for c, f in zip(cell, first)]
         keep = [split_two(x) for x in here[0:2]]
         slope = [split_two(x) for x in here[2:4]]
         values = [[v[q] for v in pair] for pair in (keep, slope) for q in range(2)]
-        for part in range(SUB):
+        for part in range(GROUP):
             row = lambda v: jnp.concatenate([x[part : part + 1, :] for x in v], axis=1)
             lanes = pl.ds(part * capacity, capacity)
             two_hot[:, lanes] = jnp.where(row(second) == two_table, 1.0, 0.0).astype(bf16)
@@ -403,13 +409,13 @@
                 one_hot[pl.ds(q * cells_one, cells_one), lanes] = mine * value
         scatter[...] += nt_dot(one_hot[...], two_hot[...])
 
-    groups = devices // SUB
+    groups = devices // GROUP
     def late_step(index, carry):
-        arrive(index * SUB, SUB, index)
+        arrive(index * GROUP, GROUP, index)
         apply_step(index)
         return carry
 
-    arrive(1, SUB - 1, 0)
+    arrive(1, GROUP - 1, 0)
     apply_step(0)
     lax.fori_loop(1, groups, late_step, 0)
 
@@ -432,10 +438,10 @@
             device_id=(my_row, my_col), device_id_type=MESH,
         ).wait_send()
 
-    sent(1, SUB - 1, 0)
+    sent(1, GROUP - 1, 0)
 
     def sent_step(index, carry):
-        sent(index * SUB, SUB, index)
+        sent(index * GROUP, GROUP, index)
         return carry
 
     lax.fori_loop(1, groups, sent_step, 0)
@@ -481,10 +487,10 @@
             half(chunks, devices, CHUNK), half(chunks, capacity, CHUNK),
             half(4 * devices, CHUNK), half(4 * devices, CHUNK), vmem(4 * devices, capacity), wide(4, sections),
             vmem(devices, 6, LANES), vmem(devices, 6, LANES),
-            half(8 * height, SUB * capacity), half(256, SUB * capacity), vmem(8 * height, 256),
+            half(8 * height, GROUP * capacity), half(256, GROUP * capacity), vmem(8 * height, 256),
             pltpu.SemaphoreType.REGULAR,
             dma(n_row - 1), dma(n_row - 1), dma(n_row - 1), dma(n_row - 1),
-            dma(devices // SUB), dma(devices // SUB), dma(8), dma(8), dma(8), dma(8), dma(14),
+            dma(devices // GROUP), dma(devices // GROUP), dma(8), dma(8), dma(8), dma(8), dma(14),
         ],
         compiler_params=pltpu.CompilerParams(
             collective_id=0, has_side_effects=True, vmem_limit_bytes=60 << 20

time: 46.7 us -> 44.8 us (0.959)
  Pallas kernels: 45.9 us -> 44 us
    pallas_call x1, Pallas kernels: 43.6 us -> 41.7 us  [whole_step(): pl.pallas_call(functools.partial(step_kernel, n_row, n_col), out_shape=(j...]
where the time goes in v4:
time: 44.8 us; the launch traced here: 44.7 us
  Pallas kernels  44 us (98%)
  between operations  0.64 us (1%)
    pallas_call x1, Pallas kernels, whole_step(): pl.pallas_call(functools.partial(step_kernel, n_row, n_col), out_shape=(j...  41.7 us
    pallas_call x1, Pallas kernels, flood(): pl.pallas_call(functools.partial(flood_kernel, n_row, n_col), out_shape=(...  2.3 us

profile of v4, /device:TPU:1, one launch (start us, length us, event | category | flops | bytes accessed | tf_op | source)
XLA Modules:
  0.0 44.7 jit_solution(12890500743222885447)
XLA Ops:
  0.6 41.7 %step.1 = (f32[16,16,128]{2,1,0:T(8,128)}, f32[5,48,768]{2,1,0:T(8,128)}) custom-call(f32[16,2,16,128]{3,2,1,0:T(8,128)} %bitcast.26, f32[16,2,16,128]{3,2,1,0:T(8,128)} %bitcast.27, f32[16,2,16,128]{3,2,1,0:T(8,128)} %bitcast.28, f32[16,16,128]{2,1,0:T(8,128)} %bitcast.29, f32[16,1024]{1,0:T(8,128)} %refs_4_.1, s32[16,1024]{1,0:T(8,128)} %refs_5_.1, ...), custom_call_target="tpu_custom_call" | custom-call | tf_op jit(solution)/shard_map/step/pallas_call | solution.py:473
  42.4 2.3 %flood.1 = (f32[32,512]{1,0:T(8,128)}, f32[32,512]{1,0:T(8,128)}, f32[32,512]{1,0:T(8,128)}, f32[16,16,128]{2,1,0:T(8,128)}) custom-call(f32[5,48,768]{2,1,0:T(8,128)} %get-tuple-element.10.field, f32[16,16,128]{2,1,0:T(8,128)} %get-tuple-element.11.state_ref), custom_call_target="tpu_custom_call" | custom-call | tf_op jit(solution)/shard_map/flood/pallas_call | solution.py:543

commit v5 on v4

--- a/solution.py
+++ b/solution.py
@@ -154,13 +154,13 @@
 def step_kernel(
     n_row, n_col, *refs
 ):
-    inputs, (state_ref, field), fetched = refs[:14], refs[14:16], refs[16:30]
+    inputs, (state_out, depth_out, one_out, two_out), fetched = refs[:14], refs[14:18], refs[18:32]
     (
-    couple, local, heads, head_in, edges, edge_in, crest, regime, cells, tiles, earlier,
+    state_ref, field, couple, local, heads, head_in, edges, edge_in, crest, regime, cells, tiles, earlier,
     hot, ranks, left, left_two, total, pieces, slots, land, one_hot, two_hot, scatter,
     ready, send_one, recv_one, send_two, recv_two, send_all, recv_all,
-    send_fix, recv_fix, send_wet, recv_wet, fetch,
-    ) = refs[30:]
+    send_fix, recv_fix, send_wet, recv_wet, fetch, store,
+    ) = refs[32:]
     (
         lower_ref, main_ref, upper_ref, rhs_ref, crest_ref, regime_ref, tile_ref, row_ref, col_ref,
         bed_ref, depth_ref, one_ref, two_ref, mask_ref,
@@ -300,9 +300,9 @@
         return sent
 
     pl.semaphore_wait(ready, n_col - 1)
-    fixed = halo(pl.ds(1, 4), send_fix, recv_fix)
     lax.fori_loop(first_part, chunks // 2, rank_step, offset)
     multiply(left_two, chunks - 1, 2)
+    fixed = halo(pl.ds(1, 4), send_fix, recv_fix)
 
     def build(left, index, source, extent):
         for part in range(CHUNK // wide):
@@ -377,6 +377,10 @@
 
     lax.fori_loop(1, devices, send_step, 0)
     land[0] = slots[0]
+    for copy in fixed:
+        copy.wait()
+    stored = pltpu.make_async_copy(state_ref, state_out, store.at[0])
+    stored.start()
 
     cells_one, cells_two = 2 * height, 256
     scatter[...] = jnp.zeros_like(scatter)
@@ -445,8 +449,10 @@
         return carry
 
     lax.fori_loop(1, groups, sent_step, 0)
-    for copy in fixed + wet:
+    for copy in wet:
         copy.wait()
+    flood_steps(n_row, n_col, field, depth_out, one_out, two_out)
+    stored.wait()
 
 
 def dense(x):
@@ -474,12 +480,13 @@
         functools.partial(step_kernel, n_row, n_col),
         out_shape=(
             jax.ShapeDtypeStruct((sections, 2 * SUB, LANES), f32),
-            jax.ShapeDtypeStruct((5, height + 2 * SUB, width + 2 * LANES), f32),
-        ),
+        )
+        + (jax.ShapeDtypeStruct((height, width), f32),) * 3,
         in_specs=[HBM_SPEC] * 14,
-        out_specs=(VMEM_SPEC,) * 2,
+        out_specs=(HBM_SPEC,) + (VMEM_SPEC,) * 3,
         scratch_shapes=[pltpu.VMEM(x.shape, x.dtype) for x in operands]
         + [
+            vmem(sections, 2 * SUB, LANES), vmem(5, height + 2 * SUB, width + 2 * LANES),
             wide(sections, 4), wide(sections, 10),
             vmem(n_row, 24, LANES), vmem(n_row, 24, LANES), wide(n_row), wide(n_row),
             wide(sections), pltpu.VMEM((sections, SUB, LANES), i32), wide(2, sections),
@@ -490,7 +497,7 @@
             half(8 * height, GROUP * capacity), half(256, GROUP * capacity), vmem(8 * height, 256),
             pltpu.SemaphoreType.REGULAR,
             dma(n_row - 1), dma(n_row - 1), dma(n_row - 1), dma(n_row - 1),
-            dma(devices // GROUP), dma(devices // GROUP), dma(8), dma(8), dma(8), dma(8), dma(14),
+            dma(devices // GROUP), dma(devices // GROUP), dma(8), dma(8), dma(8), dma(8), dma(14), dma(1),
         ],
         compiler_params=pltpu.CompilerParams(
             collective_id=0, has_side_effects=True, vmem_limit_bytes=60 << 20
@@ -506,8 +513,7 @@
     return pushed / (1.0 + (GRAVITY * TIME_STEP * MANNING_SQ) * jnp.abs(old) * drag)
 
 
-def flood_kernel(n_row, n_col, field, state_ref, depth_out, one_out, two_out, state_out):
-    state_out[...] = state_ref[...]
+def flood_steps(n_row, n_col, field, depth_out, one_out, two_out):
     height, width = depth_out.shape
     my_row, my_col = lax.axis_index("row"), lax.axis_index("col")
     depth, bed, one, two, mask = [field[q] for q in range(5)]
@@ -539,22 +545,26 @@
     two_out[...] = two[inner]
 
 
-def flood(field, state, shape, n_row, n_col):
+def hand_over_kernel(*refs):
+    count = len(refs) // 2
+    for source, target in zip(refs[:count], refs[count:]):
+        target[...] = source[...]
+
+
+def hand_over(*arrays):
     return pl.pallas_call(
-        functools.partial(flood_kernel, n_row, n_col),
-        out_shape=(jax.ShapeDtypeStruct(shape, f32),) * 3
-        + (jax.ShapeDtypeStruct(state.shape, f32),),
-        in_specs=[VMEM_SPEC] * 2,
-        out_specs=(VMEM_SPEC,) * 4,
-        name="flood",
-    )(field, state)
+        hand_over_kernel,
+        out_shape=tuple(jax.ShapeDtypeStruct(x.shape, x.dtype) for x in arrays),
+        in_specs=[VMEM_SPEC] * len(arrays),
+        out_specs=(VMEM_SPEC,) * len(arrays),
+        name="hand_over",
+    )(*arrays)
 
 
 def local_step(*args):
     n_row, n_col = lax.axis_size("row"), lax.axis_size("col")
-    rhs, bed = args[3], args[9]
-    state, field = whole_step(args, n_row, n_col)
-    depth, one, two, state = flood(field, state, bed.shape, n_row, n_col)
+    rhs = args[3]
+    state, depth, one, two = hand_over(*whole_step(args, n_row, n_col))
     state = jnp.swapaxes(state.reshape(-1, SUB, 2, LANES), 1, 2).reshape(rhs.shape)
     return (state, depth, one, two)
 

time: 44.8 us -> 44.5 us (level)
    pallas_call x1, Pallas kernels: 2.3 us -> 1.69 us  [hand_over(): pl.pallas_call(hand_over_kernel, out_shape=tuple((jax.ShapeDtypeStruct(x....]
where the time goes in v5:
time: 44.5 us; the launch traced here: 44.4 us
  Pallas kernels  43.7 us (98%)
  between operations  0.64 us (1%)
    pallas_call x1, Pallas kernels, whole_step(): pl.pallas_call(functools.partial(step_kernel, n_row, n_col), out_shape=(j...  42 us
    pallas_call x1, Pallas kernels, hand_over(): pl.pallas_call(hand_over_kernel, out_shape=tuple((jax.ShapeDtypeStruct(x....  1.69 us

profile of v5, /device:TPU:1, one launch (start us, length us, event | category | flops | bytes accessed | tf_op | source)
XLA Modules:
  0.0 44.4 jit_solution(758675217240435733)
XLA Ops:
  0.6 42.0 %step.1 = (f32[16,16,128]{2,1,0:T(8,128)}, f32[32,512]{1,0:T(8,128)}, f32[32,512]{1,0:T(8,128)}, f32[32,512]{1,0:T(8,128)}) custom-call(f32[16,2,16,128]{3,2,1,0:T(8,128)} %bitcast.26, f32[16,2,16,128]{3,2,1,0:T(8,128)} %bitcast.27, f32[16,2,16,128]{3,2,1,0:T(8,128)} %bitcast.28, f32[16,16,128]{2,1,0:T(8,128)} %bitcast.29, f32[16,1024]{1,0:T(8,128)} %refs_4_.1, ...), custom_call_target="tpu_custom_call" | custom-call | tf_op jit(solution)/shard_map/step/pallas_call | solution.py:479
  42.7 1.7 %hand_over.1 = (f32[16,16,128]{2,1,0:T(8,128)}, f32[32,512]{1,0:T(8,128)}, f32[32,512]{1,0:T(8,128)}, f32[32,512]{1,0:T(8,128)}) custom-call(f32[16,16,128]{2,1,0:T(8,128)} %get-tuple-element.12.refs_0_, f32[32,512]{1,0:T(8,128)} %get-tuple-element.13.refs_1_, f32[32,512]{1,0:T(8,128)} %get-tuple-element.14.refs_2_, f32[32,512]{1,0:T(8,128)} %get-tuple-element.15.refs_3_), custom_call_target="tpu_custom_call" | custom-call | tf_op jit(solution)/shard_map/hand_over/pallas_call | solution.py:555
